TPU v7x, 512 devices: a whole 4x8x8 slice. The times are simulated.
512 devices in a mesh: pipe: 8 (over y_lo, core), tensor: 64 (over y_hi, x, z).
Axes of the slice: x: 4, y: 8 (y_hi: 2, y_lo: 4; y = y_hi * 4 + y_lo), z: 8, core: 2. Of those that a mesh axis runs over, the one named last changes fastest.
Arguments:
- output_gradient: bfloat16 [8, 64, 2, 64, 1024], P('pipe', 'tensor'), may hold values from -6 to 6
- forward_input: bfloat16 [8, 2, 512, 8192], P('pipe', None, None, 'tensor'), may hold values from -6 to 6
- saved_rank_outputs: bfloat16 [8, 2, 512, 64], P('pipe', None, 'tensor'), may hold values from -6 to 6
- projection_weight: bfloat16 [8, 64, 1024, 1024], P('pipe', 'tensor'), may hold values from -0.0625 to 0.0625
- adapter_down_maps: bfloat16 [8, 8, 64, 8192], P('pipe', None, None, 'tensor'), may hold values from -0.75 to 0.75
- adapter_up_maps: bfloat16 [8, 64, 8, 8, 1024], P('pipe', 'tensor'), may hold values from -0.0625 to 0.0625
- segment_adapter_class: int32 [8, 2, 4], P('pipe'), may hold values from 0 to 7
- live_segment_table: int32 [8, 2], P('pipe'), may hold values from 1 to 4, as said below
Outputs:
- grad_prev: bfloat16 [8, 2, 512, 8192], P('pipe', None, None, 'tensor')
- down_map_gradient: bfloat16 [8, 8, 64, 8192], P('pipe', None, None, 'tensor')
- up_map_gradient: bfloat16 [8, 64, 8, 8, 1024], P('pipe', 'tensor')
Inputs may be any that keep to these rules, and one draw needn't show every extreme that they name: The first live_segment_table segments of a microbatch are live; some microbatch has all 4 live.
All inputs are finite; a program needn't handle non-finite values.
Results may differ from a plain program's by a relative error of at most 0.0049.
Values may be sent and summed in bfloat16 or wider, within the bound.
A program may use at most 64 MiB of HBM per device.

v0:
```python
import jax
import jax.numpy as jnp
from jax import lax
from jax.sharding import PartitionSpec as P

SEG = 128


def partner(value, axis, apart):
    mask = 2**apart
    pairs = [(source, source ^ mask) for source in range(lax.axis_size(axis))]
    return lax.ppermute(value, axis, pairs)


def shifted(block, axis, distance):
    devices = range(lax.axis_size(axis))
    route = [((i - distance) % len(devices), i) for i in devices]
    return lax.ppermute(block, axis, route)


def choose_segment_rows(class_indicator, segment_lookup):
    return jnp.einsum(
        "pzw,wlq->pzlq", class_indicator, segment_lookup, preferred_element_type=jnp.float32
    ).astype(jnp.bfloat16)


def shards(
    output_gradient,
    forward_input,
    saved_rank_outputs,
    projection_weight,
    adapter_down_maps,
    adapter_up_maps,
    segment_adapter_class,
    live_segment_table,
):
    grad_tile = output_gradient[0, 0]
    micro_count, tile_rows, tile_cols = grad_tile.shape
    weight = projection_weight[0, 0]
    up_matrix_tile = adapter_up_maps[0, 0]
    rank_part = up_matrix_tile.shape[1]
    rank_extent = adapter_down_maps.shape[2]
    local_portion = adapter_down_maps.shape[3]
    group_size = lax.axis_size("tensor")
    total_bits = group_size.bit_length() - 1
    low_size = min(group_size, 8)
    low_bits = low_size.bit_length() - 1
    high_size = group_size // low_size
    position = lax.axis_index("tensor")
    high_index = position // low_size
    batch_rows = tile_rows * high_size
    seg_count = batch_rows // SEG
    row_ids = high_index * tile_rows + jnp.arange(tile_rows, dtype=jnp.int32)
    live_count = live_segment_table[0]
    keep_rows = (row_ids // SEG)[None, :] < live_count[:, None]
    masked_tile = jnp.where(keep_rows[:, :, None], grad_tile, jnp.zeros_like(grad_tile))
    gathered = masked_tile
    for level in range(low_bits, total_bits):
        received = partner(gathered, "tensor", level)
        leading = position >> level & 1 == 0
        gathered = jnp.where(
            leading,
            jnp.concatenate([gathered, received], 1),
            jnp.concatenate([received, gathered], 1),
        )
    products = jnp.einsum("mrd,id->mri", gathered, weight, preferred_element_type=jnp.float32)
    reduced = products
    for level in reversed(range(low_bits)):
        half_cols = reduced.shape[2] // 2
        lower_half = reduced[:, :, :half_cols]
        upper_half = reduced[:, :, half_cols:]
        upper_side = position >> level & 1 == 1
        kept_half = jnp.where(upper_side, upper_half, lower_half)
        sent_half = jnp.where(upper_side, lower_half, upper_half)
        reduced = kept_half + partner(sent_half, "tensor", level)
    classes = segment_adapter_class[0]
    class_indicator = (
        classes[:, :, None] == jnp.arange(up_matrix_tile.shape[0], dtype=jnp.int32)[None, None, :]
    ).astype(jnp.bfloat16)
    selected_up_matrix = choose_segment_rows(class_indicator, up_matrix_tile)
    grad_segs = gathered.reshape(micro_count, seg_count, SEG, tile_cols)
    partial_rank = jnp.einsum(
        "mskd,msrd->mskr", grad_segs, selected_up_matrix, preferred_element_type=jnp.float32
    )
    padded_rank = jnp.zeros((micro_count, seg_count, SEG, rank_extent), jnp.float32)
    padded_rank = lax.dynamic_update_slice_in_dim(
        padded_rank, partial_rank, high_index * rank_part, 3
    )
    lowrank = lax.psum(padded_rank, "tensor").astype(jnp.bfloat16)
    selected_down_matrix = choose_segment_rows(class_indicator, adapter_down_maps[0])
    adapter = jnp.einsum(
        "mskr,msrd->mskd", lowrank, selected_down_matrix, preferred_element_type=jnp.float32
    )
    input_gradient = (reduced + adapter.reshape(micro_count, batch_rows, local_portion)).astype(
        jnp.bfloat16
    )
    grad_prev = shifted(input_gradient, "pipe", -1)
    inputs_seg = forward_input[0].reshape(micro_count, seg_count, SEG, local_portion)
    segment_down_matrix = jnp.einsum(
        "mskr,mskd->msrd", lowrank, inputs_seg, preferred_element_type=jnp.float32
    )
    hidden = lax.all_gather(saved_rank_outputs[0], "tensor", axis=1, tiled=True)
    hidden_part = lax.dynamic_slice_in_dim(hidden, high_index * rank_part, rank_part, 2)
    hidden_seg = hidden_part.reshape(micro_count, seg_count, SEG, rank_part)
    segment_up_matrix = jnp.einsum(
        "mskr,mskd->msrd", hidden_seg, grad_segs, preferred_element_type=jnp.float32
    )
    wide_class_indicator = class_indicator.astype(jnp.float32)
    down_map_gradient = jnp.einsum(
        "exk,exlq->klq", wide_class_indicator, segment_down_matrix, precision=lax.Precision.HIGHEST
    ).astype(jnp.bfloat16)
    up_map_gradient = jnp.einsum(
        "exk,exlq->klq", wide_class_indicator, segment_up_matrix, precision=lax.Precision.HIGHEST
    ).astype(jnp.bfloat16)
    return (grad_prev[None], down_map_gradient[None], up_map_gradient[None, None])


def solution(mesh):
    in_specs = (
        P("pipe", "tensor", None, None, None),
        P("pipe", None, None, "tensor"),
        P("pipe", None, "tensor", None),
        P("pipe", "tensor", None, None),
        P("pipe", None, None, "tensor"),
        P("pipe", "tensor", None, None, None),
        P("pipe", None, None),
        P("pipe", None),
    )
    out_specs = (
        P("pipe", None, None, "tensor"),
        P("pipe", None, None, "tensor"),
        P("pipe", "tensor", None, None, None),
    )
    return jax.shard_map(shards, mesh=mesh, in_specs=in_specs, out_specs=out_specs, check_vma=False)
```

profile of v0, /device:TPU:1, one launch (start us, length us, event | category | flops | bytes accessed | tf_op | source)
XLA Modules:
  0.0 876.1 jit_solution(1295151885727014478)
XLA Ops:
  0.7 0.9 broadcast_compare_fusion
  1.5 1.0 bitcast_select_fusion
  2.6 3.9 collective-permute-start
  6.5 3.7 collective-permute-done
  10.4 6.9 collective-permute-start.1
  17.3 9.1 %collective-permute-done.1 = bf16[2,128,1024]{2,1,0:T(8,128)(2,1)} collective-permute-done((bf16[2,128,1024]{2,1,0:T(8,128)(2,1)S(1)}, bf16[2,128,1024]{2,1,0:T(8,128)(2,1)}, u32[]{:S(2)}, u32[]{:S(2)}) %collective-permute-start.1) | collective-permute-done | bytes 524320 | tf_op jit(solution)/shard_map/ppermute | solution.py:12
  26.4 2.1 maximum_select_fusion.1
  28.4 9.2 %collective-permute-start.2 = (bf16[2,256,1024]{2,1,0:T(8,128)(2,1)S(1)}, bf16[2,256,1024]{2,1,0:T(8,128)(2,1)}, u32[]{:S(2)}, u32[]{:S(2)}) collective-permute-start(bf16[2,256,1024]{2,1,0:T(8,128)(2,1)S(1)} %maximum_select_fusion.1), channel_id=1, source_target_pairs={{0,32},{1,33},{2,34},{3,35},{4,36},{5,37},{6,38},{7,39},{8,40},{9,... | collective-permute-start | bytes 3145736 | tf_op jit(solution)/shard_map/ppermute | solution.py:12
  37.6 30.7 %collective-permute-done.2 = bf16[2,256,1024]{2,1,0:T(8,128)(2,1)} collective-permute-done((bf16[2,256,1024]{2,1,0:T(8,128)(2,1)S(1)}, bf16[2,256,1024]{2,1,0:T(8,128)(2,1)}, u32[]{:S(2)}, u32[]{:S(2)}) %collective-permute-start.2) | collective-permute-done | bytes 1048608 | tf_op jit(solution)/shard_map/ppermute | solution.py:12
  68.3 2.6 maximum_select_fusion
  70.9 2.4 fusion
  73.3 2.2 slice_select_fusion
  76.1 10.7 %collective-permute-start.3 = (f32[2,512,512]{2,1,0:T(8,128)}, f32[2,512,512]{2,1,0:T(8,128)}, u32[]{:S(2)}, u32[]{:S(2)}) collective-permute-start(f32[2,512,512]{2,1,0:T(8,128)} %slice_select_fusion), channel_id=1, source_target_pairs={{0,4},{1,5},{2,6},{3,7},{4,0},{5,1},{6,2},{7,3},{8,12},{9,13},{10,... | collective-permute-start | bytes 6291464 | tf_op jit(solution)/shard_map/ppermute | solution.py:12
  86.8 273.6 %all-gather = bf16[1,2,512,64]{3,2,1,0:T(8,128)(2,1)S(1)} all-gather(bf16[1,2,8,64]{3,2,1,0:T(8,128)(2,1)S(1)} %copy-done.12), channel_id=2, replica_groups=mesh['pipe'=8,'tensor'=64] {'tensor'}, dimensions={2}, use_global_device_ids=true | all-gather | bytes 133120 | tf_op jit(solution)/shard_map/all_gather | solution.py:102
  360.4 3.6 select_add_fusion
  364.0 1.3 copy-done.3
  365.5 1.9 collective-permute-start.4
  367.6 0.9 fusion.10
  368.5 1.1 fusion.12
  369.7 2.4 convolution_dynamic-update-slice_fusion
  372.1 0.7 copy-done.7
  373.2 11.7 %collective-permute-done.4 = f32[2,512,256]{2,1,0:T(8,128)} collective-permute-done((f32[2,512,256]{2,1,0:T(8,128)S(1)}, f32[2,512,256]{2,1,0:T(8,128)}, u32[]{:S(2)}, u32[]{:S(2)}) %collective-permute-start.4) | collective-permute-done | bytes 1048608 | tf_op jit(solution)/shard_map/ppermute | solution.py:12
  384.9 1.4 select_add_fusion.1
  386.3 0.8 slice_select_fusion.2
  387.2 1.9 collective-permute-start.5
  389.7 0.7 copy.12
  390.4 374.0 %all-reduce.1 = bf16[2,4,128,64]{2,3,1,0:T(8,128)(2,1)S(1)} all-reduce(f32[2,4,128,64]{2,3,1,0:T(8,128)S(1)} %copy-done.8), channel_id=1, replica_groups=mesh['pipe'=8,'tensor'=64] {'tensor'}, use_global_device_ids=true, to_apply=%region_0.1 | all-reduce | flops 65536 | bytes 393216 | tf_op jit(solution)/shard_map/psum | solution.py:89
  764.4 1.2 fusion.9
  765.6 1.2 fusion.6
  766.8 92.6 %collective-permute-start.6 = (bf16[2,512,128]{2,1,0:T(8,128)(2,1)S(1)}, bf16[2,512,128]{2,1,0:T(8,128)(2,1)S(1)}, u32[]{:S(2)}, u32[]{:S(2)}) collective-permute-start(bf16[2,512,128]{2,1,0:T(8,128)(2,1)S(1)} %fusion.6), channel_id=1, source_target_pairs={{64,0},{128,64},{192,128},{256,192},{320,256},{384,320},{448,384},... | collective-permute-start | bytes 786440 | tf_op jit(solution)/shard_map/ppermute | solution.py:18
  860.9 14.5 %collective-permute-done.6 = bf16[2,512,128]{2,1,0:T(8,128)(2,1)S(1)} collective-permute-done((bf16[2,512,128]{2,1,0:T(8,128)(2,1)S(1)}, bf16[2,512,128]{2,1,0:T(8,128)(2,1)S(1)}, u32[]{:S(2)}, u32[]{:S(2)}) %collective-permute-start.6) | collective-permute-done | bytes 262176 | tf_op jit(solution)/shard_map/ppermute | solution.py:18
  875.4 0.7 copy.38
  (36 shorter events, 3.5 us)
Async XLA Ops:
  0.6 70.3 %copy-start = (bf16[1,1,1024,1024]{3,2,1,0:T(8,128)(2,1)S(1)}, bf16[1,1,1024,1024]{3,2,1,0:T(8,128)(2,1)}, u32[]{:S(2)}) copy-start(bf16[1,1,1024,1024]{3,2,1,0:T(8,128)(2,1)} %param.11) | copy-start | bytes 6291460
  2.6 7.7 collective-permute-start
  10.4 6.9 copy-start.6
  10.4 15.9 %collective-permute-start.1 = (bf16[2,128,1024]{2,1,0:T(8,128)(2,1)S(1)}, bf16[2,128,1024]{2,1,0:T(8,128)(2,1)}, u32[]{:S(2)}, u32[]{:S(2)}) collective-permute-start(bf16[2,128,1024]{2,1,0:T(8,128)(2,1)S(1)} %maximum_select_fusion.2), channel_id=1, source_target_pairs={{0,16},{1,17},{2,18},{3,19},{4,20},{5,21},{6,22},{7,23},{8,24},{9,... | collective-permute-start | bytes 1572872 | tf_op jit(solution)/shard_map/ppermute | solution.py:12
  28.4 39.9 %collective-permute-start.2 = (bf16[2,256,1024]{2,1,0:T(8,128)(2,1)S(1)}, bf16[2,256,1024]{2,1,0:T(8,128)(2,1)}, u32[]{:S(2)}, u32[]{:S(2)}) collective-permute-start(bf16[2,256,1024]{2,1,0:T(8,128)(2,1)S(1)} %maximum_select_fusion.1), channel_id=1, source_target_pairs={{0,32},{1,33},{2,34},{3,35},{4,36},{5,37},{6,38},{7,39},{8,40},{9,... | collective-permute-start | bytes 3145736 | tf_op jit(solution)/shard_map/ppermute | solution.py:12
  70.9 2.4 copy-start.1
  73.3 2.7 copy-start.5
  73.3 13.4 %copy-start.12 = (bf16[1,2,8,64]{3,2,1,0:T(8,128)(2,1)S(1)}, bf16[1,2,8,64]{3,2,1,0:T(8,128)(2,1)}, u32[]{:S(2)}) copy-start(bf16[1,2,8,64]{3,2,1,0:T(8,128)(2,1)} %param.10) | copy-start | bytes 6148
  76.1 284.3 %collective-permute-start.3 = (f32[2,512,512]{2,1,0:T(8,128)}, f32[2,512,512]{2,1,0:T(8,128)}, u32[]{:S(2)}, u32[]{:S(2)}) collective-permute-start(f32[2,512,512]{2,1,0:T(8,128)} %slice_select_fusion), channel_id=1, source_target_pairs={{0,4},{1,5},{2,6},{3,7},{4,0},{5,1},{6,2},{7,3},{8,12},{9,13},{10,... | collective-permute-start | bytes 6291464 | tf_op jit(solution)/shard_map/ppermute | solution.py:12
  364.0 1.3 copy-start.3
  365.3 2.2 copy-start.10
  365.3 2.2 copy-start.11
  365.5 19.4 %collective-permute-start.4 = (f32[2,512,256]{2,1,0:T(8,128)S(1)}, f32[2,512,256]{2,1,0:T(8,128)}, u32[]{:S(2)}, u32[]{:S(2)}) collective-permute-start(f32[2,512,256]{2,1,0:T(8,128)S(1)} %slice_select_fusion.1), channel_id=1, source_target_pairs={{0,2},{1,3},{2,0},{3,1},{4,6},{5,7},{6,4},{7,5},{8,10},{9,11},{10,... | collective-permute-start | bytes 3145736 | tf_op jit(solution)/shard_map/ppermute | solution.py:12
  367.6 5.2 copy-start.2
  369.7 15.2 %copy-start.4 = (f32[2,512,512]{2,1,0:T(8,128)S(1)}, f32[2,512,512]{2,1,0:T(8,128)}, u32[]{:S(2)}) copy-start(f32[2,512,512]{2,1,0:T(8,128)} %copy-done.3) | copy-start | bytes 6291460
  372.1 0.7 copy-start.7
  386.3 4.1 copy-start.8
  387.2 378.4 %collective-permute-start.5 = (f32[2,512,128]{2,1,0:T(8,128)}, f32[2,512,128]{2,1,0:T(8,128)}, u32[]{:S(2)}, u32[]{:S(2)}) collective-permute-start(f32[2,512,128]{2,1,0:T(8,128)} %slice_select_fusion.2), channel_id=1, source_target_pairs={{0,1},{1,0},{2,3},{3,2},{4,5},{5,4},{6,7},{7,6},{8,9},{9,8},{10,11... | collective-permute-start | bytes 1572872 | tf_op jit(solution)/shard_map/ppermute | solution.py:12
  764.4 95.1 %copy-start.9 = (bf16[1,2,512,128]{3,2,1,0:T(8,128)(2,1)S(1)}, bf16[1,2,512,128]{3,2,1,0:T(8,128)(2,1)}, u32[]{:S(2)}) copy-start(bf16[1,2,512,128]{3,2,1,0:T(8,128)(2,1)} %param.9) | copy-start | bytes 786436
  766.8 108.6 %collective-permute-start.6 = (bf16[2,512,128]{2,1,0:T(8,128)(2,1)S(1)}, bf16[2,512,128]{2,1,0:T(8,128)(2,1)S(1)}, u32[]{:S(2)}, u32[]{:S(2)}) collective-permute-start(bf16[2,512,128]{2,1,0:T(8,128)(2,1)S(1)} %fusion.6), channel_id=1, source_target_pairs={{64,0},{128,64},{192,128},{256,192},{320,256},{384,320},{448,384},... | collective-permute-start | bytes 786440 | tf_op jit(solution)/shard_map/ppermute | solution.py:18
where the time goes:
time: 878 us; the launch traced here: 876 us
  blocking collectives  648 us (74%)
  starting transfers between devices  127 us (14%)
  waiting for transfers between devices  69.6 us (8%)
  other arithmetic  16.1 us (2%)
  matrix products  9.78 us (1%)
    psum x1, blocking collectives, shards(): lowrank = lax.psum(padded_rank, 'tensor').astype(jnp.bfloat16)  374 us
    all_gather x1, blocking collectives, shards(): hidden = lax.all_gather(saved_rank_outputs[0], 'tensor', axis=1, tiled=True)  274 us
    ppermute x1, starting transfers between devices, shifted(): return lax.ppermute(block, axis, route)  92.6 us
    ppermute x6, waiting for transfers between devices, partner(): return lax.ppermute(value, axis, pairs)  55.1 us
    ppermute x6, starting transfers between devices, partner(): return lax.ppermute(value, axis, pairs)  34.5 us
  transfers between devices with their start and end apart: 7, of which 5 were waited for; matrix products, arithmetic and copies ran while one was open for 1% of the time, Pallas kernels for 0%

commit v1 on v0

v1 whole, which is shorter than its diff:
```python
import jax
import jax.numpy as jnp
from jax import lax
from jax.experimental import pallas as pl
from jax.experimental.pallas import tpu as pltpu
from jax.sharding import PartitionSpec as P

MESH = pl.DeviceIdType.MESH
BF = jnp.bfloat16
F32 = jnp.float32
NX, NZ, NH, NP = 4, 8, 8, 8
ROWS = 64
LAG = 2
ORDER = (
    "O0", "O1", "L0", "R1", "L1", "R0", "X0", "X1",
    "Y0", "YL0", "YR0", "YX0", "Y1", "YL1", "YR1", "YX1",
)
SLOT = {name: i for i, name in enumerate(ORDER)}
N = len(ORDER)
SHIFT = {"O": 0, "L": 3, "R": 1, "X": 2, "Y": 0, "YL": 3, "YR": 1, "YX": 2}
ONWARD = {
    "L0": ((1, "X0"),),
    "R1": ((-1, "X1"),),
    "Y0": ((1, "YL0"), (-1, "YR0")),
    "Y1": ((1, "YL1"), (-1, "YR1")),
    "YL0": ((1, "YX0"),),
    "YR1": ((-1, "YX1"),),
}
EARLY = {6: ("Y0",), 11: ("Y1",)}
T_UP, T_SUM, T_SPREAD, T_RANK, T_DU, T_DA = 5, 8, 11, 17, 16, 18


def nt(a, b):
    return lax.dot_general(a, b, (((1,), (1,)), ((), ())), preferred_element_type=F32)


def nn(a, b):
    return lax.dot_general(a, b, (((1,), (0,)), ((), ())), preferred_element_type=F32)


def section(
    cls_ref, live_ref, g_ref, x_ref, hid_ref, w_ref, a_ref, u_ref,
    out_ref, da_ref, du_ref,
    gall, wv, pbuf, zs, zr, uf, us, ug, plb, plr, l2b, l2r, l3b, lfull, lt,
    hz, hkb, hk, xv, av, fin, dacc,
    loc, gss, grs, zss, zrs, uss, urs, l1s, l1r, l2s, l2rs, l3s, l3r, h1s, h1r, h2s, h2r, fs, fr,
):
    p = lax.axis_index("pipe")
    t = lax.axis_index("tensor")
    z = lax.rem(t, NZ)
    h = t // NZ
    x = lax.rem(h, NX)
    yh = h // NX

    def at_z(j):
        return (p, h * NZ + lax.rem(z + j + NZ, NZ))

    def at_h(j):
        return (p, lax.rem(h + j + NH, NH) * NZ + z)

    def at_x(j):
        return (p, (yh * NX + lax.rem(x + j + NX, NX)) * NZ + z)

    at_y = (p, ((1 - yh) * NX + x) * NZ + z)
    before = (lax.rem(p + NP - 1, NP), t)
    after = (lax.rem(p + 1, NP), t)

    def rows_of(name):
        shift = SHIFT[name[:-1]]
        there = 1 - yh if name[0] == "Y" else yh
        return there * NX + lax.rem(x + shift, NX), int(name[-1])

    bar = pltpu.get_barrier_semaphore()
    for j in range(1, NZ):
        pl.semaphore_signal(bar, inc=1, device_id=at_z(j), device_id_type=MESH)
    for j in range(1, NH):
        pl.semaphore_signal(bar, inc=1, device_id=at_h(j), device_id_type=MESH)
    pl.semaphore_signal(bar, inc=1, device_id=before, device_id_type=MESH)
    pl.semaphore_signal(bar, inc=1, device_id=after, device_id_type=MESH)

    loads = [
        pltpu.make_async_copy(g_ref.at[0], gall.at[0], loc.at[0]),
        pltpu.make_async_copy(g_ref.at[1], gall.at[1], loc.at[1]),
        pltpu.make_async_copy(w_ref, wv, loc.at[2]),
        pltpu.make_async_copy(x_ref, xv, loc.at[3]),
        pltpu.make_async_copy(a_ref, av, loc.at[4]),
    ]
    for load in loads:
        load.start()

    uf[...] = u_ref[...].astype(F32).reshape(uf.shape)
    for s in range(4):
        us[s] = jnp.concatenate([uf[cls_ref[s]], uf[cls_ref[4 + s]]], 0).astype(BF)
    ug[h] = us[h // 2]
    hz[z] = hid_ref[...]

    pl.semaphore_wait(bar, 16)

    sends = []

    def remote(src, dst, ssem, rsem, where):
        return pltpu.make_async_remote_copy(
            src_ref=src, dst_ref=dst, send_sem=ssem, recv_sem=rsem,
            device_id=where, device_id_type=MESH,
        )

    def send(*args):
        copy = remote(*args)
        copy.start()
        sends.append(copy)

    def g_send(src, k, where, name):
        send(src, gall.at[SLOT[name]], gss.at[k], grs.at[SLOT[name]], where)

    g_send(g_ref.at[0], 0, at_x(1), "L0")
    g_send(g_ref.at[1], 1, at_x(-1), "R1")
    g_send(g_ref.at[0], 2, at_y, "Y0")
    g_send(g_ref.at[1], 3, at_x(1), "L1")
    g_send(g_ref.at[0], 4, at_x(-1), "R0")
    for j in range(1, NH):
        there = lax.rem(h + j, NH)
        send(us.at[there // 2], ug.at[h], uss.at[j], urs.at[j], at_h(j))
    g_send(g_ref.at[1], 5, at_y, "Y1")
    for j in range(1, NZ):
        send(hid_ref, hz.at[z], h1s.at[j], h1r.at[j], at_z(j))
    count = [6]
    here = set()

    def arrive(name):
        if name in here:
            return
        here.add(name)
        slot = SLOT[name]
        if slot < 2:
            loads[slot].wait()
        else:
            remote(gall.at[slot], gall.at[slot], gss.at[0], grs.at[slot], at_y).wait_recv()
        for direction, name_there in ONWARD.get(name, ()):
            g_send(gall.at[slot], count[0], at_x(direction), name_there)
            count[0] += 1

    def hop(c, s):
        for d, sign in ((0, 1), (1, -1)):
            k = d * 4 + s - 1
            block = lax.rem(z + sign * (5 - s) + NZ, NZ)
            if s == 1:
                lo = 32 * d
                zs[c, k, 0:32, :] = pbuf[c, block, lo:lo + 32, :].astype(BF)
                src, dst = zs.at[c, k, 0:32], zr.at[c, k, 0:32]
            else:
                q = k - 1
                if s == 2:
                    got = zr.at[c, q, 0:32]
                else:
                    got = zr.at[c, q]
                remote(got, got, zss.at[c, q], zrs.at[c, q], at_z(sign)).wait_recv()
                if s == 2:
                    lo = 32 * d
                    other = 32 - lo
                    zs[c, k, lo:lo + 32, :] = (
                        pbuf[c, block, lo:lo + 32, :] + zr[c, q, 0:32, :].astype(F32)
                    ).astype(BF)
                    zs[c, k, other:other + 32, :] = pbuf[c, block, other:other + 32, :].astype(BF)
                else:
                    zs[c, k] = (pbuf[c, block] + zr[c, q].astype(F32)).astype(BF)
                src, dst = zs.at[c, k], zr.at[c, k]
            send(src, dst, zss.at[c, k], zrs.at[c, k], at_z(sign))

    lane = lax.broadcasted_iota(jnp.int32, (8, 128), 1)

    def of_block(b, table):
        return jnp.where(lane < ROWS, table(0, b // 2), table(1, b // 2))

    def class_or_none(m, s):
        return jnp.where(s < live_ref[m], cls_ref[m * 4 + s], -1)

    def alive(m, s):
        return jnp.where(s < live_ref[m], 1, 0)

    def emit(c):
        b, m = rows_of(ORDER[c])
        fin[c] = pbuf[c, z].astype(BF)
        send(
            fin.at[c], out_ref.at[m, pl.ds(pl.multiple_of(b * ROWS, ROWS), ROWS)],
            fs.at[c], fr.at[c], before,
        )

    adapters_in = [False]

    def finish(c):
        for q in (3, 7):
            remote(zr.at[c, q], zr.at[c, q], zss.at[c, q], zrs.at[c, q], at_z(1)).wait_recv()
        b, m = rows_of(ORDER[c])
        keep = jnp.zeros((ROWS, 128), jnp.int32) + alive(m, b // 2)
        total = pbuf[c, z] + zr[c, 3].astype(F32) + zr[c, 7].astype(F32)
        total = jnp.where(keep > 0, total, 0.0)
        if adapters_in[0]:
            total = total + lt[c]
        pbuf[c, z] = total
        if adapters_in[0]:
            emit(c)

    def up_rows():
        for j in range(1, NH):
            src = lax.rem(h - j + NH, NH)
            remote(ug.at[src], ug.at[src], uss.at[j], urs.at[j], at_h(j)).wait_recv()
        own = jnp.concatenate([gall[0], gall[1]], 0)
        both = nt(ug[...].reshape(128, 1024), own).reshape(8, 2, 8, 128)
        keep = of_block(h, alive)[None] > 0
        part = jnp.where(lane[None] < ROWS, both[:, 0], both[:, 1])
        plb[...] = jnp.where(keep, part, 0.0)
        plr[z] = plb[z]
        for j in range(1, NZ):
            there = lax.rem(z + j, NZ)
            send(plb.at[there], plr.at[z], l1s.at[j], l1r.at[j], at_z(j))

    def rank_sum():
        for j in range(1, NZ):
            src = lax.rem(z - j + NZ, NZ)
            remote(plr.at[src], plr.at[src], l1s.at[j], l1r.at[j], at_z(j)).wait_recv()
        total = jnp.sum(plr[...], 0).astype(BF).astype(F32)
        l2b[...] = total
        l2r[z] = total
        for j in range(1, NZ):
            send(l2b, l2r.at[z], l2s.at[j], l2rs.at[j], at_z(j))
        for j in range(1, NZ):
            src = lax.rem(z - j + NZ, NZ)
            remote(hz.at[src], hz.at[src], h1s.at[j], h1r.at[j], at_z(j)).wait_recv()
        hv = hz[...].astype(F32)
        hv = jnp.concatenate([hv[:, 0].reshape(64, 64), hv[:, 1].reshape(64, 64)], 0).astype(BF)
        r = lax.broadcasted_iota(jnp.int32, (64, 64), 0)
        c = lax.broadcasted_iota(jnp.int32, (64, 64), 1)
        hkb[...] = nt(jnp.where(r == c, 1.0, 0.0).astype(BF), hv).reshape(8, 8, 128)
        hk[h] = hkb[h]
        for j in range(1, NH):
            there = lax.rem(h + j, NH)
            send(hkb.at[there], hk.at[h], h2s.at[j], h2r.at[j], at_h(j))

    def rank_spread():
        for j in range(1, NZ):
            src = lax.rem(z - j + NZ, NZ)
            remote(l2r.at[src], l2r.at[src], l2s.at[j], l2rs.at[j], at_z(j)).wait_recv()
        mine = l2r[...].reshape(64, 128).astype(BF)
        l3b[...] = mine
        lfull[h] = mine
        for j in range(1, NH):
            send(l3b, lfull.at[h], l3s.at[j], l3r.at[j], at_h(j))

    def rank_here(done):
        for j in range(1, NH):
            src = lax.rem(h - j + NH, NH)
            remote(lfull.at[src], lfull.at[src], l3s.at[j], l3r.at[j], at_h(j)).wait_recv()
        loads[4].wait()
        r = lax.broadcasted_iota(jnp.int32, (128, 128), 0)
        c = lax.broadcasted_iota(jnp.int32, (128, 128), 1)
        eye = jnp.where(r == c, 1.0, 0.0).astype(BF)
        for name in ("O", "L", "R", "X", "Y", "YL", "YR", "YX"):
            b, _ = rows_of(name + "0")
            turned = nt(eye, lfull[b]).astype(BF)
            for m in range(2):
                slot = SLOT[name + str(m)]
                term = nn(turned[m * ROWS:(m + 1) * ROWS], av[cls_ref[m * 4 + b // 2]])
                if slot in done:
                    pbuf[slot, z] = pbuf[slot, z] + term
                else:
                    lt[slot] = term
        adapters_in[0] = True
        for slot in done:
            emit(slot)

    def up_gradient():
        for j in range(1, NH):
            src = lax.rem(h - j + NH, NH)
            remote(hk.at[src], hk.at[src], h2s.at[j], h2r.at[j], at_h(j)).wait_recv()
        number = lax.broadcasted_iota(jnp.int32, (8, 8, 128), 0)
        left, right = [], []
        for name in ("O", "L", "R", "X", "Y", "YL", "YR", "YX"):
            b, _ = rows_of(name + "0")
            chosen = of_block(b, class_or_none)[None]
            left.append(jnp.where(number == chosen, hk[b][None], 0.0).reshape(64, 128).astype(BF))
            right.append(gall[SLOT[name + "0"]])
            right.append(gall[SLOT[name + "1"]])
        du_ref[...] = nn(jnp.concatenate(left, 1), jnp.concatenate(right, 0)).astype(BF)

    def down_gradient():
        loads[3].wait()
        number = lax.broadcasted_iota(jnp.int32, (8, 64, 128), 0)
        for b in range(NH):
            wide = lax.broadcasted_iota(jnp.int32, (64, 128), 1)
            chosen = jnp.where(wide < ROWS, class_or_none(0, b // 2), class_or_none(1, b // 2))[None]
            left = jnp.where(number == chosen, lfull[b].astype(F32)[None], 0.0)
            left = left.reshape(512, 128).astype(BF)
            right = jnp.concatenate(
                [xv[0, b * ROWS:(b + 1) * ROWS], xv[1, b * ROWS:(b + 1) * ROWS]], 0
            )
            part = nn(left, right)
            if b == 0:
                dacc[...] = part
            elif b < NH - 1:
                dacc[...] += part
            else:
                da_ref[...] = (dacc[...] + part).astype(BF)

    loads[2].wait()
    done = []
    for step in range(N + 4 * LAG):
        if 0 <= step - 4 * LAG < N:
            finish(step - 4 * LAG)
            if not adapters_in[0]:
                done.append(step - 4 * LAG)
        for s in (4, 3, 2):
            if 0 <= step - LAG * (s - 1) < N:
                hop(step - LAG * (s - 1), s)
        for name in EARLY.get(step, ()):
            arrive(name)
        if step < N:
            arrive(ORDER[step])
            prod = nt(gall[step], wv[...])
            for j in range(NZ):
                pbuf[step, j] = prod[:, j * 128:(j + 1) * 128]
            hop(step, 1)
        if step == T_UP:
            up_rows()
        if step == T_SUM:
            rank_sum()
        if step == T_SPREAD:
            rank_spread()
        if step == T_RANK:
            rank_here(tuple(done))
        if step == T_DU:
            up_gradient()
        if step == T_DA:
            down_gradient()

    for c in range(N):
        b, m = rows_of(ORDER[c])
        dst = out_ref.at[m, pl.ds(pl.multiple_of(b * ROWS, ROWS), ROWS)]
        remote(fin.at[c], dst, fs.at[c], fr.at[c], before).wait_recv()
    for copy in sends:
        copy.wait_send()


def shards(
    output_gradient, forward_input, saved_rank_outputs, projection_weight,
    adapter_down_maps, adapter_up_maps, segment_adapter_class, live_segment_table,
):
    vm = pltpu.VMEM
    dma = pltpu.SemaphoreType.DMA
    smem = pl.BlockSpec(memory_space=pltpu.SMEM)
    vmem = pl.BlockSpec(memory_space=pltpu.VMEM)
    hbm = pl.BlockSpec(memory_space=pl.ANY)
    out, da, du = pl.pallas_call(
        section,
        name="section",
        out_shape=(
            jax.ShapeDtypeStruct((2, 512, 128), BF),
            jax.ShapeDtypeStruct((512, 128), BF),
            jax.ShapeDtypeStruct((64, 1024), BF),
        ),
        in_specs=[smem, smem, hbm, hbm, vmem, hbm, hbm, vmem],
        out_specs=(vmem, vmem, vmem),
        scratch_shapes=[
            vm((N, ROWS, 1024), BF), vm((1024, 1024), BF), vm((N, 8, ROWS, 128), F32),
            vm((N, 8, ROWS, 128), BF), vm((N, 8, ROWS, 128), BF),
            vm((8, 8, 1024), F32), vm((4, 16, 1024), BF), vm((8, 16, 1024), BF),
            vm((8, 8, 128), F32), vm((8, 8, 128), F32), vm((8, 128), F32), vm((8, 8, 128), F32),
            vm((64, 128), BF), vm((8, 64, 128), BF), vm((N, ROWS, 128), F32),
            vm((8, 2, 8, 64), BF), vm((8, 8, 128), F32), vm((8, 8, 128), F32),
            vm((2, 512, 128), BF), vm((8, 64, 128), BF), vm((N, ROWS, 128), BF), vm((512, 128), F32),
            dma((5,)), dma((16,)), dma((N,)), dma((N, 8)), dma((N, 8)),
            dma((8,)), dma((8,)), dma((8,)), dma((8,)), dma((8,)), dma((8,)),
            dma((8,)), dma((8,)), dma((8,)), dma((8,)), dma((8,)), dma((8,)), dma((N,)), dma((N,)),
        ],
        compiler_params=pltpu.CompilerParams(
            collective_id=0, has_side_effects=True, vmem_limit_bytes=48 * 1024 * 1024
        ),
    )(
        segment_adapter_class.reshape(8),
        live_segment_table.reshape(2),
        output_gradient.reshape(2, ROWS, 1024),
        forward_input.reshape(2, 512, 128),
        saved_rank_outputs.reshape(2, 8, 64),
        projection_weight.reshape(1024, 1024),
        adapter_down_maps.reshape(8, 64, 128),
        adapter_up_maps.reshape(64, 1024),
    )
    return (
        out.reshape(1, 2, 512, 128),
        da.reshape(1, 8, 64, 128),
        du.reshape(1, 1, 8, 8, 1024),
    )


def solution(mesh):
    in_specs = (
        P("pipe", "tensor", None, None, None),
        P("pipe", None, None, "tensor"),
        P("pipe", None, "tensor", None),
        P("pipe", "tensor", None, None),
        P("pipe", None, None, "tensor"),
        P("pipe", "tensor", None, None, None),
        P("pipe", None, None),
        P("pipe", None),
    )
    out_specs = (
        P("pipe", None, None, "tensor"),
        P("pipe", None, None, "tensor"),
        P("pipe", "tensor", None, None, None),
    )
    return jax.shard_map(shards, mesh=mesh, in_specs=in_specs, out_specs=out_specs, check_vma=False)
```

time: 878 us -> 84.3 us (0.10)
  blocking collectives: 648 us -> 0 us
  starting transfers between devices: 127 us -> 0 us
  Pallas kernels: 0 us -> 73.3 us
  waiting for transfers between devices: 69.6 us -> 0 us
  other arithmetic: 16.1 us -> 0 us
  matrix products: 9.78 us -> 0 us
    psum x1 -> x0, blocking collectives: 374 us -> none  [shards(): lowrank = lax.psum(padded_rank, 'tensor').astype(jnp.bfloat16)]
    all_gather x1 -> x0, blocking collectives: 274 us -> none  [shards(): hidden = lax.all_gather(saved_rank_outputs[0], 'tensor', axis=1, tiled=True)]
    ppermute x7 -> x0, starting transfers between devices: 127 us -> none  [the longest x1 92.6 us: shifted(): return lax.ppermute(block, axis, route)]
    pallas_call x0 -> x1, Pallas kernels: none -> 73.3 us  [shards(): pl.pallas_call(section, name='section', out_shape=(jax.ShapeDtypeStruct((...]
    ppermute x7 -> x0, waiting for transfers between devices: 69.6 us -> none  [the longest x6 55.1 us: partner(): return lax.ppermute(value, axis, pairs)]
    dot_general x9 -> x0, matrix products: 9.78 us -> none  [the longest x1 2.39 us: shards(): jnp.einsum('mskd,msrd->mskr', grad_segs, selected_up_matrix, preferred_el...]
    select_n x8 -> x0, other arithmetic: 9 us -> none  [the longest x3 4.79 us: shards(): jnp.where(leading, jnp.concatenate([gathered, received], 1), jnp.concaten...]
  transfers between devices with their start and end apart: 7 -> 0, of which waited for: 5 -> 0; matrix products, arithmetic and copies ran while one was open for 1% -> 0% of each run, Pallas kernels for 0% -> 0%
where the time goes in v1:
time: 84.3 us; the launch traced here: 83.4 us
  Pallas kernels  73.3 us (87%)
  local copies, waits for them, and re-layouts  9.41 us (11%)
    pallas_call x1, Pallas kernels, shards(): pl.pallas_call(section, name='section', out_shape=(jax.ShapeDtypeStruct((...  73.3 us
    unnamed x17, local copies, waits for them, and re-layouts  8.65 us

profile of v1, /device:TPU:1, one launch (start us, length us, event | category | flops | bytes accessed | tf_op | source)
XLA Modules:
  0.0 83.4 jit_solution(6922491261872380157)
XLA Ops:
  0.6 0.8 reshape.39.cls_ref
  1.4 0.0 copy-start
  1.4 1.6 %copy-done = bf16[1,1,1024,1024]{3,2,1,0:T(8,128)(2,1)S(1)} copy-done((bf16[1,1,1024,1024]{3,2,1,0:T(8,128)(2,1)S(1)}, bf16[1,1,1024,1024]{3,2,1,0:T(8,128)(2,1)}, u32[]{:S(2)}) %copy-start) | copy-done | bytes 2097176
  3.0 0.0 copy-start.1
  3.0 0.9 %copy-done.1 = bf16[1,1,2,64,1024]{4,3,2,1,0:T(8,128)(2,1)S(1)} copy-done((bf16[1,1,2,64,1024]{4,3,2,1,0:T(8,128)(2,1)S(1)}, bf16[1,1,2,64,1024]{4,3,2,1,0:T(8,128)(2,1)}, u32[]{:S(2)}) %copy-start.1) | copy-done | bytes 262168
  3.9 0.0 copy-start.2
  3.9 0.9 %copy-done.2 = bf16[1,2,512,128]{3,2,1,0:T(8,128)(2,1)S(1)} copy-done((bf16[1,2,512,128]{3,2,1,0:T(8,128)(2,1)S(1)}, bf16[1,2,512,128]{3,2,1,0:T(8,128)(2,1)}, u32[]{:S(2)}) %copy-start.2) | copy-done | bytes 262168
  4.9 0.0 copy-start.3
  4.9 0.9 %copy-done.3 = bf16[1,8,64,128]{3,2,1,0:T(8,128)(2,1)S(1)} copy-done((bf16[1,8,64,128]{3,2,1,0:T(8,128)(2,1)S(1)}, bf16[1,8,64,128]{3,2,1,0:T(8,128)(2,1)}, u32[]{:S(2)}) %copy-start.3) | copy-done | bytes 131096
  5.8 0.0 copy-start.4
  5.8 0.9 %copy-done.4 = bf16[1,1,8,8,1024]{4,3,2,1,0:T(8,128)(2,1)S(1)} copy-done((bf16[1,1,8,8,1024]{4,3,2,1,0:T(8,128)(2,1)S(1)}, bf16[1,1,8,8,1024]{4,3,2,1,0:T(8,128)(2,1)}, u32[]{:S(2)}) %copy-start.4) | copy-done | bytes 131096
  6.7 0.0 copy-start.5
  6.7 0.7 copy-done.5
  7.4 0.0 copy-start.6
  7.4 0.7 copy-done.6
  8.0 73.3 %section.1 = (bf16[2,512,128]{2,1,0:T(8,128)(2,1)S(1)}, bf16[512,128]{1,0:T(8,128)(2,1)S(1)}, bf16[64,1024]{1,0:T(8,128)(2,1)S(1)}) custom-call(s32[8]{0:T(128)S(1)} %reshape.39.cls_ref, s32[2]{0:T(128)S(1)} %bitcast.19, bf16[2,64,1024]{2,1,0:T(8,128)(2,1)S(1)} %bitcast.12, bf16[2,512,128]{2,1,0:T(8,128)(2,1)S(1)} %bitcast.13, ...), custom_call_target="tpu_custom_call" | custom-call | tf_op jit(solution)/shard_map/section/pallas_call | solution.py:352
  81.3 0.7 copy.14
  82.0 0.7 copy.15
  82.7 0.7 copy.16
Async XLA Ops:
  1.4 1.6 %copy-start = (bf16[1,1,1024,1024]{3,2,1,0:T(8,128)(2,1)S(1)}, bf16[1,1,1024,1024]{3,2,1,0:T(8,128)(2,1)}, u32[]{:S(2)}) copy-start(bf16[1,1,1024,1024]{3,2,1,0:T(8,128)(2,1)} %param.11) | copy-start | bytes 6291460
  3.0 0.9 %copy-start.1 = (bf16[1,1,2,64,1024]{4,3,2,1,0:T(8,128)(2,1)S(1)}, bf16[1,1,2,64,1024]{4,3,2,1,0:T(8,128)(2,1)}, u32[]{:S(2)}) copy-start(bf16[1,1,2,64,1024]{4,3,2,1,0:T(8,128)(2,1)} %param.8) | copy-start | bytes 786436
  3.9 0.9 %copy-start.2 = (bf16[1,2,512,128]{3,2,1,0:T(8,128)(2,1)S(1)}, bf16[1,2,512,128]{3,2,1,0:T(8,128)(2,1)}, u32[]{:S(2)}) copy-start(bf16[1,2,512,128]{3,2,1,0:T(8,128)(2,1)} %param.9) | copy-start | bytes 786436
  4.9 0.9 %copy-start.3 = (bf16[1,8,64,128]{3,2,1,0:T(8,128)(2,1)S(1)}, bf16[1,8,64,128]{3,2,1,0:T(8,128)(2,1)}, u32[]{:S(2)}) copy-start(bf16[1,8,64,128]{3,2,1,0:T(8,128)(2,1)} %param.12) | copy-start | bytes 393220
  5.8 0.9 %copy-start.4 = (bf16[1,1,8,8,1024]{4,3,2,1,0:T(8,128)(2,1)S(1)}, bf16[1,1,8,8,1024]{4,3,2,1,0:T(8,128)(2,1)}, u32[]{:S(2)}) copy-start(bf16[1,1,8,8,1024]{4,3,2,1,0:T(8,128)(2,1)} %param.13) | copy-start | bytes 393220
  6.7 0.7 copy-start.5
  7.4 0.7 copy-start.6

commit v2 on v1

--- a/solution.py
+++ b/solution.py
@@ -10,24 +10,37 @@
 F32 = jnp.float32
 NX, NZ, NH, NP = 4, 8, 8, 8
 ROWS = 64
-LAG = 2
+LAG = 4
 ORDER = (
-    "O0", "O1", "L0", "R1", "L1", "R0", "X0", "X1",
-    "Y0", "YL0", "YR0", "YX0", "Y1", "YL1", "YR1", "YX1",
+    "O0", "O1", "L0", "R0", "L1", "R1", "X0", "X1",
+    "Y0", "YL0", "YR0", "Y1", "YX0", "YL1", "YR1", "YX1",
 )
 SLOT = {name: i for i, name in enumerate(ORDER)}
 N = len(ORDER)
+LAST = N - 1
 SHIFT = {"O": 0, "L": 3, "R": 1, "X": 2, "Y": 0, "YL": 3, "YR": 1, "YX": 2}
 ONWARD = {
-    "L0": ((1, "X0"),),
-    "R1": ((-1, "X1"),),
-    "Y0": ((1, "YL0"), (-1, "YR0")),
-    "Y1": ((1, "YL1"), (-1, "YR1")),
-    "YL0": ((1, "YX0"),),
-    "YR1": ((-1, "YX1"),),
+    ("L0", 0): ((1, "X0"),),
+    ("L1", 0): ((1, "X1"),),
+    ("R0", 1): ((-1, "X0"),),
+    ("R1", 1): ((-1, "X1"),),
+    ("Y0", 0): ((1, "YL0"), (-1, "YR0")),
+    ("Y0", 1): ((1, "YL0"), (-1, "YR0")),
+    ("Y1", 0): ((1, "YL1"), (-1, "YR1")),
+    ("Y1", 1): ((1, "YL1"), (-1, "YR1"), (2, "YX1")),
+    ("YL0", 0): ((1, "YX0"),),
+    ("YL1", 0): ((1, "YX1"),),
+    ("YR0", 1): ((-1, "YX0"),),
 }
-EARLY = {6: ("Y0",), 11: ("Y1",)}
-T_UP, T_SUM, T_SPREAD, T_RANK, T_DU, T_DA = 5, 8, 11, 17, 16, 18
+EARLY = {
+    7: (("Y0", 0),),
+    9: (("YL0", 0), ("Y1", 0)),
+    12: (("YL1", 0),),
+}
+EVENTS = {
+    "up_relay": 3, "up_rows": 7, "rank_sum": 10, "rank_spread": 12, "rank_relay": 15,
+    "up_gradient": 17, "rank_here": 23, "down_gradient": 26,
+}
 
 
 def nt(a, b):
@@ -42,8 +55,8 @@
     cls_ref, live_ref, g_ref, x_ref, hid_ref, w_ref, a_ref, u_ref,
     out_ref, da_ref, du_ref,
     gall, wv, pbuf, zs, zr, uf, us, ug, plb, plr, l2b, l2r, l3b, lfull, lt,
-    hz, hkb, hk, xv, av, fin, dacc,
-    loc, gss, grs, zss, zrs, uss, urs, l1s, l1r, l2s, l2rs, l3s, l3r, h1s, h1r, h2s, h2r, fs, fr,
+    hz, hkb, hk, xv, av, fin, dacc, uv, hidv, uy, hy, zd, zdr,
+    loc, gss, grs, zss, zrs, uss, urs, l1s, l1r, l2s, l2rs, l3s, l3r, h1s, h1r, h2s, h2r, fs, fr, zds, zdrs,
 ):
     p = lax.axis_index("pipe")
     t = lax.axis_index("tensor")
@@ -55,13 +68,15 @@
     def at_z(j):
         return (p, h * NZ + lax.rem(z + j + NZ, NZ))
 
-    def at_h(j):
-        return (p, lax.rem(h + j + NH, NH) * NZ + z)
-
     def at_x(j):
         return (p, (yh * NX + lax.rem(x + j + NX, NX)) * NZ + z)
 
-    at_y = (p, ((1 - yh) * NX + x) * NZ + z)
+    hp = (1 - yh) * NX + x
+    at_y = (p, hp * NZ + z)
+
+    def from_x(j):
+        return yh * NX + lax.rem(x - j + NX, NX), (1 - yh) * NX + lax.rem(x - j + NX, NX)
+
     before = (lax.rem(p + NP - 1, NP), t)
     after = (lax.rem(p + 1, NP), t)
 
@@ -73,12 +88,15 @@
     bar = pltpu.get_barrier_semaphore()
     for j in range(1, NZ):
         pl.semaphore_signal(bar, inc=1, device_id=at_z(j), device_id_type=MESH)
-    for j in range(1, NH):
-        pl.semaphore_signal(bar, inc=1, device_id=at_h(j), device_id_type=MESH)
+    for j in range(1, NX):
+        pl.semaphore_signal(bar, inc=1, device_id=at_x(j), device_id_type=MESH)
+    pl.semaphore_signal(bar, inc=1, device_id=at_y, device_id_type=MESH)
     pl.semaphore_signal(bar, inc=1, device_id=before, device_id_type=MESH)
     pl.semaphore_signal(bar, inc=1, device_id=after, device_id_type=MESH)
 
     loads = [
+        pltpu.make_async_copy(u_ref, uv, loc.at[5]),
+        pltpu.make_async_copy(hid_ref, hidv, loc.at[6]),
         pltpu.make_async_copy(g_ref.at[0], gall.at[0], loc.at[0]),
         pltpu.make_async_copy(g_ref.at[1], gall.at[1], loc.at[1]),
         pltpu.make_async_copy(w_ref, wv, loc.at[2]),
@@ -87,14 +105,16 @@
     ]
     for load in loads:
         load.start()
-
-    uf[...] = u_ref[...].astype(F32).reshape(uf.shape)
+    loads.pop(0).wait()
+    loads.pop(0).wait()
+
+    uf[...] = uv[...].astype(F32).reshape(uf.shape)
     for s in range(4):
-        us[s] = jnp.concatenate([uf[cls_ref[s]], uf[cls_ref[4 + s]]], 0).astype(BF)
+        us[s] = jnp.concatenate([uf[cls_ref[0, 0, s]], uf[cls_ref[0, 1, s]]], 0).astype(BF)
     ug[h] = us[h // 2]
-    hz[z] = hid_ref[...]
-
-    pl.semaphore_wait(bar, 16)
+    hz[z] = hidv[...]
+
+    pl.semaphore_wait(bar, 13)
 
     sends = []
 
@@ -109,35 +129,49 @@
         copy.start()
         sends.append(copy)
 
-    def g_send(src, k, where, name):
-        send(src, gall.at[SLOT[name]], gss.at[k], grs.at[SLOT[name]], where)
-
-    g_send(g_ref.at[0], 0, at_x(1), "L0")
-    g_send(g_ref.at[1], 1, at_x(-1), "R1")
-    g_send(g_ref.at[0], 2, at_y, "Y0")
-    g_send(g_ref.at[1], 3, at_x(1), "L1")
-    g_send(g_ref.at[0], 4, at_x(-1), "R0")
-    for j in range(1, NH):
-        there = lax.rem(h + j, NH)
-        send(us.at[there // 2], ug.at[h], uss.at[j], urs.at[j], at_h(j))
-    g_send(g_ref.at[1], 5, at_y, "Y1")
+    count = [0]
+
+    def g_send(src, where, name, half):
+        slot = SLOT[name]
+        dst = gall.at[slot, pl.ds(32 * half, 32)]
+        send(src, dst, gss.at[count[0]], grs.at[slot, half], where)
+        count[0] += 1
+
+    def own(m, half):
+        return g_ref.at[m, pl.ds(32 * half, 32)]
+
+    send(us.at[pl.ds(2 * (1 - yh), 2)], uy, uss.at[0], urs.at[0], at_y)
+    for m in range(2):
+        for half in range(2):
+            g_send(own(m, half), at_x(1), f"L{m}", half)
+            g_send(own(m, half), at_x(-1), f"R{m}", half)
+            g_send(own(m, half), at_y, f"Y{m}", half)
     for j in range(1, NZ):
-        send(hid_ref, hz.at[z], h1s.at[j], h1r.at[j], at_z(j))
-    count = [6]
+        send(hidv, hz.at[z], h1s.at[j], h1r.at[j], at_z(j))
+    for j in range(1, NX):
+        there = lax.rem(x + j, NX)
+        send(us.at[2 * yh + there // 2], ug.at[h], uss.at[j], urs.at[j], at_x(j))
     here = set()
 
-    def arrive(name):
-        if name in here:
-            return
-        here.add(name)
+    def arrive(name, halves=(0, 1)):
         slot = SLOT[name]
-        if slot < 2:
-            loads[slot].wait()
-        else:
-            remote(gall.at[slot], gall.at[slot], gss.at[0], grs.at[slot], at_y).wait_recv()
-        for direction, name_there in ONWARD.get(name, ()):
-            g_send(gall.at[slot], count[0], at_x(direction), name_there)
-            count[0] += 1
+        for half in halves:
+            if (name, half) in here:
+                continue
+            here.add((name, half))
+            got = gall.at[slot, pl.ds(32 * half, 32)]
+            if slot < 2:
+                if half == 0:
+                    loads[slot].wait()
+            else:
+                remote(got, got, gss.at[0], grs.at[slot, half], at_y).wait_recv()
+            for direction, name_there in ONWARD.get((name, half), ()):
+                g_send(got, at_x(direction), name_there, half)
+
+    def direct():
+        for j in (4, 3, 5, 2, 6, 1, 7):
+            zd[j] = pbuf[LAST, lax.rem(z + j, NZ)].astype(BF)
+            send(zd.at[j], zdr.at[z], zds.at[j], zdrs.at[j], at_z(j))
 
     def hop(c, s):
         for d, sign in ((0, 1), (1, -1)):
@@ -172,10 +206,10 @@
         return jnp.where(lane < ROWS, table(0, b // 2), table(1, b // 2))
 
     def class_or_none(m, s):
-        return jnp.where(s < live_ref[m], cls_ref[m * 4 + s], -1)
+        return jnp.where(s < live_ref[0, m], cls_ref[0, m, s], -1)
 
     def alive(m, s):
-        return jnp.where(s < live_ref[m], 1, 0)
+        return jnp.where(s < live_ref[0, m], 1, 0)
 
     def emit(c):
         b, m = rows_of(ORDER[c])
@@ -188,11 +222,18 @@
     adapters_in = [False]
 
     def finish(c):
-        for q in (3, 7):
-            remote(zr.at[c, q], zr.at[c, q], zss.at[c, q], zrs.at[c, q], at_z(1)).wait_recv()
+        if c == LAST:
+            total = pbuf[c, z]
+            for j in (1, 7, 2, 6, 3, 5, 4):
+                src = lax.rem(z - j + NZ, NZ)
+                remote(zdr.at[src], zdr.at[src], zds.at[j], zdrs.at[j], at_z(j)).wait_recv()
+                total = total + zdr[src].astype(F32)
+        else:
+            for q in (3, 7):
+                remote(zr.at[c, q], zr.at[c, q], zss.at[c, q], zrs.at[c, q], at_z(1)).wait_recv()
+            total = pbuf[c, z] + zr[c, 3].astype(F32) + zr[c, 7].astype(F32)
         b, m = rows_of(ORDER[c])
         keep = jnp.zeros((ROWS, 128), jnp.int32) + alive(m, b // 2)
-        total = pbuf[c, z] + zr[c, 3].astype(F32) + zr[c, 7].astype(F32)
         total = jnp.where(keep > 0, total, 0.0)
         if adapters_in[0]:
             total = total + lt[c]
@@ -200,10 +241,17 @@
         if adapters_in[0]:
             emit(c)
 
+    def up_relay():
+        remote(uy, uy, uss.at[0], urs.at[0], at_y).wait_recv()
+        for j in range(1, NX):
+            there = lax.rem(x + j, NX)
+            send(uy.at[there // 2], ug.at[hp], uss.at[3 + j], urs.at[3 + j], at_x(j))
+        ug[hp] = uy[x // 2]
+
     def up_rows():
-        for j in range(1, NH):
-            src = lax.rem(h - j + NH, NH)
-            remote(ug.at[src], ug.at[src], uss.at[j], urs.at[j], at_h(j)).wait_recv()
+        for j in range(1, NX):
+            for k, src in zip((j, 3 + j), from_x(j)):
+                remote(ug.at[src], ug.at[src], uss.at[k], urs.at[k], at_x(j)).wait_recv()
         own = jnp.concatenate([gall[0], gall[1]], 0)
         both = nt(ug[...].reshape(128, 1024), own).reshape(8, 2, 8, 128)
         keep = of_block(h, alive)[None] > 0
@@ -232,9 +280,10 @@
         c = lax.broadcasted_iota(jnp.int32, (64, 64), 1)
         hkb[...] = nt(jnp.where(r == c, 1.0, 0.0).astype(BF), hv).reshape(8, 8, 128)
         hk[h] = hkb[h]
-        for j in range(1, NH):
-            there = lax.rem(h + j, NH)
-            send(hkb.at[there], hk.at[h], h2s.at[j], h2r.at[j], at_h(j))
+        send(hkb.at[pl.ds(NX * (1 - yh), NX)], hy, h2s.at[0], h2r.at[0], at_y)
+        for j in range(1, NX):
+            there = yh * NX + lax.rem(x + j, NX)
+            send(hkb.at[there], hk.at[h], h2s.at[j], h2r.at[j], at_x(j))
 
     def rank_spread():
         for j in range(1, NZ):
@@ -243,13 +292,24 @@
         mine = l2r[...].reshape(64, 128).astype(BF)
         l3b[...] = mine
         lfull[h] = mine
-        for j in range(1, NH):
-            send(l3b, lfull.at[h], l3s.at[j], l3r.at[j], at_h(j))
+        send(l3b, lfull.at[h], l3s.at[0], l3r.at[0], at_y)
+        for j in range(1, NX):
+            send(l3b, lfull.at[h], l3s.at[j], l3r.at[j], at_x(j))
+
+    def rank_relay():
+        remote(lfull.at[hp], lfull.at[hp], l3s.at[0], l3r.at[0], at_y).wait_recv()
+        for j in range(1, NX):
+            send(lfull.at[hp], lfull.at[hp], l3s.at[3 + j], l3r.at[3 + j], at_x(j))
+        remote(hy, hy, h2s.at[0], h2r.at[0], at_y).wait_recv()
+        for j in range(1, NX):
+            there = lax.rem(x + j, NX)
+            send(hy.at[there], hk.at[hp], h2s.at[3 + j], h2r.at[3 + j], at_x(j))
+        hk[hp] = hy[x]
 
     def rank_here(done):
-        for j in range(1, NH):
-            src = lax.rem(h - j + NH, NH)
-            remote(lfull.at[src], lfull.at[src], l3s.at[j], l3r.at[j], at_h(j)).wait_recv()
+        for j in range(1, NX):
+            for k, src in zip((j, 3 + j), from_x(j)):
+                remote(lfull.at[src], lfull.at[src], l3s.at[k], l3r.at[k], at_x(j)).wait_recv()
         loads[4].wait()
         r = lax.broadcasted_iota(jnp.int32, (128, 128), 0)
         c = lax.broadcasted_iota(jnp.int32, (128, 128), 1)
@@ -259,7 +319,7 @@
             turned = nt(eye, lfull[b]).astype(BF)
             for m in range(2):
                 slot = SLOT[name + str(m)]
-                term = nn(turned[m * ROWS:(m + 1) * ROWS], av[cls_ref[m * 4 + b // 2]])
+                term = nn(turned[m * ROWS:(m + 1) * ROWS], av[cls_ref[0, m, b // 2]])
                 if slot in done:
                     pbuf[slot, z] = pbuf[slot, z] + term
                 else:
@@ -269,9 +329,9 @@
             emit(slot)
 
     def up_gradient():
-        for j in range(1, NH):
-            src = lax.rem(h - j + NH, NH)
-            remote(hk.at[src], hk.at[src], h2s.at[j], h2r.at[j], at_h(j)).wait_recv()
+        for j in range(1, NX):
+            for k, src in zip((j, 3 + j), from_x(j)):
+                remote(hk.at[src], hk.at[src], h2s.at[k], h2r.at[k], at_x(j)).wait_recv()
         number = lax.broadcasted_iota(jnp.int32, (8, 8, 128), 0)
         left, right = [], []
         for name in ("O", "L", "R", "X", "Y", "YL", "YR", "YX"):
@@ -304,32 +364,40 @@
     loads[2].wait()
     done = []
     for step in range(N + 4 * LAG):
-        if 0 <= step - 4 * LAG < N:
-            finish(step - 4 * LAG)
+        c = step - 4 * LAG
+        if 0 <= c:
+            finish(c)
             if not adapters_in[0]:
-                done.append(step - 4 * LAG)
+                done.append(c)
         for s in (4, 3, 2):
-            if 0 <= step - LAG * (s - 1) < N:
+            if 0 <= step - LAG * (s - 1) < LAST:
                 hop(step - LAG * (s - 1), s)
-        for name in EARLY.get(step, ()):
-            arrive(name)
+        for name, half in EARLY.get(step, ()):
+            arrive(name, (half,))
         if step < N:
             arrive(ORDER[step])
             prod = nt(gall[step], wv[...])
             for j in range(NZ):
                 pbuf[step, j] = prod[:, j * 128:(j + 1) * 128]
-            hop(step, 1)
-        if step == T_UP:
+            if step == LAST:
+                direct()
+            else:
+                hop(step, 1)
+        if step == EVENTS["up_relay"]:
+            up_relay()
+        if step == EVENTS["up_rows"]:
             up_rows()
-        if step == T_SUM:
+        if step == EVENTS["rank_sum"]:
             rank_sum()
-        if step == T_SPREAD:
+        if step == EVENTS["rank_spread"]:
             rank_spread()
-        if step == T_RANK:
+        if step == EVENTS["rank_relay"]:
+            rank_relay()
+        if step == EVENTS["rank_here"]:
             rank_here(tuple(done))
-        if step == T_DU:
+        if step == EVENTS["up_gradient"]:
             up_gradient()
-        if step == T_DA:
+        if step == EVENTS["down_gradient"]:
             down_gradient()
 
     for c in range(N):
@@ -357,7 +425,7 @@
             jax.ShapeDtypeStruct((512, 128), BF),
             jax.ShapeDtypeStruct((64, 1024), BF),
         ),
-        in_specs=[smem, smem, hbm, hbm, vmem, hbm, hbm, vmem],
+        in_specs=[smem, smem, hbm, hbm, hbm, hbm, hbm, hbm],
         out_specs=(vmem, vmem, vmem),
         scratch_shapes=[
             vm((N, ROWS, 1024), BF), vm((1024, 1024), BF), vm((N, 8, ROWS, 128), F32),
@@ -367,16 +435,18 @@
             vm((64, 128), BF), vm((8, 64, 128), BF), vm((N, ROWS, 128), F32),
             vm((8, 2, 8, 64), BF), vm((8, 8, 128), F32), vm((8, 8, 128), F32),
             vm((2, 512, 128), BF), vm((8, 64, 128), BF), vm((N, ROWS, 128), BF), vm((512, 128), F32),
-            dma((5,)), dma((16,)), dma((N,)), dma((N, 8)), dma((N, 8)),
+            vm((64, 1024), BF), vm((2, 8, 64), BF),
+            vm((2, 16, 1024), BF), vm((4, 8, 128), F32), vm((8, ROWS, 128), BF), vm((8, ROWS, 128), BF),
+            dma((7,)), dma((32,)), dma((N, 2)), dma((N, 8)), dma((N, 8)),
             dma((8,)), dma((8,)), dma((8,)), dma((8,)), dma((8,)), dma((8,)),
-            dma((8,)), dma((8,)), dma((8,)), dma((8,)), dma((8,)), dma((8,)), dma((N,)), dma((N,)),
+            dma((8,)), dma((8,)), dma((8,)), dma((8,)), dma((8,)), dma((8,)), dma((N,)), dma((N,)), dma((8,)), dma((8,)),
         ],
         compiler_params=pltpu.CompilerParams(
-            collective_id=0, has_side_effects=True, vmem_limit_bytes=48 * 1024 * 1024
+            collective_id=0, has_side_effects=True, vmem_limit_bytes=67043328
         ),
     )(
-        segment_adapter_class.reshape(8),
-        live_segment_table.reshape(2),
+        segment_adapter_class,
+        live_segment_table,
         output_gradient.reshape(2, ROWS, 1024),
         forward_input.reshape(2, 512, 128),
         saved_rank_outputs.reshape(2, 8, 64),

time: 84.3 us -> 76 us (0.902)
  local copies, waits for them, and re-layouts: 9.41 us -> 4.8 us
  Pallas kernels: 73.3 us -> 70.4 us
    unnamed x17 -> x3, local copies, waits for them, and re-layouts: 8.65 us -> 4.8 us
    pallas_call x1, Pallas kernels: 73.3 us -> 70.4 us  [shards(): pl.pallas_call(section, name='section', out_shape=(jax.ShapeDtypeStruct((...]
where the time goes in v2:
time: 76 us; the launch traced here: 75.8 us
  Pallas kernels  70.4 us (93%)
  local copies, waits for them, and re-layouts  4.8 us (6%)
    pallas_call x1, Pallas kernels, shards(): pl.pallas_call(section, name='section', out_shape=(jax.ShapeDtypeStruct((...  70.4 us
    unnamed x3, local copies, waits for them, and re-layouts  4.8 us

profile of v2, /device:TPU:1, one launch (start us, length us, event | category | flops | bytes accessed | tf_op | source)
XLA Modules:
  0.0 75.8 jit_solution(4224715757714189160)
XLA Ops:
  0.6 70.4 %section.1 = (bf16[2,512,128]{2,1,0:T(8,128)(2,1)}, bf16[512,128]{1,0:T(8,128)(2,1)}, bf16[64,1024]{1,0:T(8,128)(2,1)}) custom-call(s32[1,2,4]{2,1,0:T(2,128)} %cls_ref.1, s32[1,2]{1,0:T(1,128)} %live_ref.1, bf16[2,64,1024]{2,1,0:T(8,128)(2,1)} %bitcast.10, bf16[2,512,128]{2,1,0:T(8,128)(2,1)} %bitcast.11, bf16[2,8,64]{2,1,0:T(8,128)(2,1)} %bitcast.17, ...), custom_call_target="tpu_custom_call" | custom-call | tf_op jit(solution)/shard_map/section/pallas_call | solution.py:420
  71.0 1.7 %copy.14 = bf16[1,2,512,128]{3,2,1,0:T(8,128)(2,1)} copy(bf16[1,2,512,128]{3,2,1,0:T(8,128)(2,1)} %bitcast.12) | data formatting | bytes 524288
  72.7 1.6 %copy.15 = bf16[1,8,64,128]{3,2,1,0:T(8,128)(2,1)} copy(bf16[1,8,64,128]{3,2,1,0:T(8,128)(2,1)} %bitcast.16) | data formatting | bytes 262144
  74.2 1.6 %copy.16 = bf16[1,1,8,8,1024]{4,3,2,1,0:T(8,128)(2,1)} copy(bf16[1,1,8,8,1024]{4,3,2,1,0:T(8,128)(2,1)} %bitcast.15) | data formatting | bytes 262144

commit v3 on v2

--- a/solution.py
+++ b/solution.py
@@ -10,14 +10,13 @@
 F32 = jnp.float32
 NX, NZ, NH, NP = 4, 8, 8, 8
 ROWS = 64
-LAG = 4
 ORDER = (
     "O0", "O1", "L0", "R0", "L1", "R1", "X0", "X1",
     "Y0", "YL0", "YR0", "Y1", "YX0", "YL1", "YR1", "YX1",
 )
 SLOT = {name: i for i, name in enumerate(ORDER)}
 N = len(ORDER)
-LAST = N - 1
+TWO = (13, 14, 15)
 SHIFT = {"O": 0, "L": 3, "R": 1, "X": 2, "Y": 0, "YL": 3, "YR": 1, "YX": 2}
 ONWARD = {
     ("L0", 0): ((1, "X0"),),
@@ -32,15 +31,31 @@
     ("YL1", 0): ((1, "YX1"),),
     ("YR0", 1): ((-1, "YX0"),),
 }
-EARLY = {
-    7: (("Y0", 0),),
-    9: (("YL0", 0), ("Y1", 0)),
-    12: (("YL1", 0),),
-}
-EVENTS = {
-    "up_relay": 3, "up_rows": 7, "rank_sum": 10, "rank_spread": 12, "rank_relay": 15,
-    "up_gradient": 17, "rank_here": 23, "down_gradient": 26,
-}
+PLAN = (
+    ("mm", 0), ("mm", 1), ("hop", 0, 2, 0), ("hop", 0, 2, 1), ("fwd", "L0", 0), ("hop", 1, 2, 0),
+    ("hop", 1, 2, 1), ("fwd", "R0", 1), ("mm", 2), ("mm", 3), ("fwd", "L1", 0), ("hop", 0, 3, 0),
+    ("hop", 0, 3, 1), ("hop", 1, 3, 0), ("up_relay",), ("hop", 1, 3, 1), ("fwd", "R1", 1), ("mm", 4),
+    ("mm", 5), ("hop", 2, 2, 0), ("hop", 2, 2, 1), ("hop", 3, 2, 0), ("hop", 3, 2, 1), ("hop", 0, 4, 0),
+    ("fwd", "Y0", 0), ("hop", 0, 4, 1), ("hop", 1, 4, 0), ("hop", 1, 4, 1), ("mm", 6), ("hop", 4, 2, 0),
+    ("hop", 4, 2, 1), ("hop", 5, 2, 0), ("hop", 5, 2, 1), ("hop", 2, 3, 0), ("hop", 2, 3, 1),
+    ("fwd", "Y0", 1), ("mm", 8), ("hop", 3, 3, 0), ("hop", 3, 3, 1), ("fin", 0), ("up_rows",),
+    ("fwd", "YL0", 0), ("fin", 1), ("hop", 6, 2, 0), ("hop", 6, 2, 1), ("mm", 7), ("fwd", "Y1", 0),
+    ("hop", 4, 3, 0), ("hop", 2, 4, 0), ("hop", 2, 4, 1), ("hop", 4, 3, 1), ("hop", 5, 3, 0),
+    ("hop", 5, 3, 1), ("hop", 8, 2, 0), ("hop", 8, 2, 1), ("hop", 3, 4, 0), ("hop", 3, 4, 1), ("mm", 9),
+    ("fwd", "YR0", 1), ("mm", 10), ("fwd", "Y1", 1), ("mm", 11), ("fwd", "YL1", 0), ("hop", 6, 3, 0),
+    ("hop", 6, 3, 1), ("hop", 7, 2, 0), ("hop", 7, 2, 1), ("hop", 4, 4, 0), ("hop", 4, 4, 1), ("fin", 2),
+    ("hop", 5, 4, 0), ("hop", 5, 4, 1), ("mm", 12), ("rank_sum",), ("hop", 8, 3, 0), ("hop", 8, 3, 1),
+    ("hop", 9, 2, 0), ("hop", 9, 2, 1), ("hop", 10, 2, 0), ("hop", 10, 2, 1), ("hop", 11, 2, 0),
+    ("hop", 11, 2, 1), ("hop", 6, 4, 0), ("hop", 6, 4, 1), ("fin", 3), ("hop", 7, 3, 0), ("hop", 7, 3, 1),
+    ("mm", 13), ("fin", 4), ("fin", 5), ("mm", 14), ("hop", 12, 2, 0), ("hop", 12, 2, 1), ("mm", 15),
+    ("hop", 8, 4, 0), ("hop", 8, 4, 1), ("hop", 9, 3, 0), ("hop", 9, 3, 1), ("hop", 10, 3, 0),
+    ("hop", 10, 3, 1), ("hop", 11, 3, 0), ("hop", 11, 3, 1), ("fin", 6), ("hop", 7, 4, 0), ("hop", 7, 4, 1),
+    ("pair", 13, 0), ("pair", 13, 1), ("rank_relay",), ("pair", 14, 0), ("hop", 12, 3, 0), ("hop", 12, 3, 1),
+    ("pair", 14, 1), ("pair", 15, 0), ("pair", 15, 1), ("fin", 8), ("hop", 9, 4, 0), ("hop", 9, 4, 1),
+    ("hop", 10, 4, 0), ("hop", 10, 4, 1), ("hop", 11, 4, 0), ("hop", 11, 4, 1), ("fin", 7), ("hop", 12, 4, 1),
+    ("rank_here",), ("hop", 12, 4, 0), ("fin", 13), ("down_gradient",), ("fin", 14), ("fin", 9),
+    ("up_gradient",), ("fin", 10), ("fin", 11), ("fin", 15), ("fin", 12),
+)
 
 
 def nt(a, b):
@@ -52,11 +67,11 @@
 
 
 def section(
-    cls_ref, live_ref, g_ref, x_ref, hid_ref, w_ref, a_ref, u_ref,
+    cls_at, live_at, g_ref, x_ref, hid_ref, w_ref, a_ref, u_ref,
     out_ref, da_ref, du_ref,
-    gall, wv, pbuf, zs, zr, uf, us, ug, plb, plr, l2b, l2r, l3b, lfull, lt,
-    hz, hkb, hk, xv, av, fin, dacc, uv, hidv, uy, hy, zd, zdr,
-    loc, gss, grs, zss, zrs, uss, urs, l1s, l1r, l2s, l2rs, l3s, l3r, h1s, h1r, h2s, h2r, fs, fr, zds, zdrs,
+    gall, wv, pbuf, zs, zr, uf, us, ug, plb, plr, l3b, lfull, lt,
+    hz, hkb, hk, xv, av, fin, dacc, uv, hidv, uy, hy, cls_ref, live_ref,
+    loc, gss, grs, zss, zrs, uss, urs, l1s, l1r, l3s, l3r, h1s, h1r, h2s, h2r, fs, fr,
 ):
     p = lax.axis_index("pipe")
     t = lax.axis_index("tensor")
@@ -95,6 +110,8 @@
     pl.semaphore_signal(bar, inc=1, device_id=after, device_id_type=MESH)
 
     loads = [
+        pltpu.make_async_copy(cls_at, cls_ref, loc.at[7]),
+        pltpu.make_async_copy(live_at, live_ref, loc.at[8]),
         pltpu.make_async_copy(u_ref, uv, loc.at[5]),
         pltpu.make_async_copy(hid_ref, hidv, loc.at[6]),
         pltpu.make_async_copy(g_ref.at[0], gall.at[0], loc.at[0]),
@@ -105,8 +122,8 @@
     ]
     for load in loads:
         load.start()
-    loads.pop(0).wait()
-    loads.pop(0).wait()
+    for _ in range(4):
+        loads.pop(0).wait()
 
     uf[...] = uv[...].astype(F32).reshape(uf.shape)
     for s in range(4):
@@ -168,37 +185,49 @@
             for direction, name_there in ONWARD.get((name, half), ()):
                 g_send(got, at_x(direction), name_there, half)
 
-    def direct():
-        for j in (4, 3, 5, 2, 6, 1, 7):
-            zd[j] = pbuf[LAST, lax.rem(z + j, NZ)].astype(BF)
-            send(zd.at[j], zdr.at[z], zds.at[j], zdrs.at[j], at_z(j))
-
-    def hop(c, s):
+    def got_z(c, q, sign, rows=ROWS):
+        got = zr.at[c, q, pl.ds(0, rows)]
+        remote(got, got, zss.at[c, q], zrs.at[c, q], at_z(sign)).wait_recv()
+        return zr[c, q, 0:rows, :].astype(F32)
+
+    def put_z(c, k, far, rows=ROWS):
+        src, dst = zs.at[c, k, pl.ds(0, rows)], zr.at[c, k, pl.ds(0, rows)]
+        send(src, dst, zss.at[c, k], zrs.at[c, k], at_z(far))
+
+    def part(c, far):
+        return pbuf.at[c, lax.rem(z + far + NZ, NZ)]
+
+    def first(c):
         for d, sign in ((0, 1), (1, -1)):
-            k = d * 4 + s - 1
-            block = lax.rem(z + sign * (5 - s) + NZ, NZ)
-            if s == 1:
-                lo = 32 * d
-                zs[c, k, 0:32, :] = pbuf[c, block, lo:lo + 32, :].astype(BF)
-                src, dst = zs.at[c, k, 0:32], zr.at[c, k, 0:32]
-            else:
-                q = k - 1
-                if s == 2:
-                    got = zr.at[c, q, 0:32]
-                else:
-                    got = zr.at[c, q]
-                remote(got, got, zss.at[c, q], zrs.at[c, q], at_z(sign)).wait_recv()
-                if s == 2:
-                    lo = 32 * d
-                    other = 32 - lo
-                    zs[c, k, lo:lo + 32, :] = (
-                        pbuf[c, block, lo:lo + 32, :] + zr[c, q, 0:32, :].astype(F32)
-                    ).astype(BF)
-                    zs[c, k, other:other + 32, :] = pbuf[c, block, other:other + 32, :].astype(BF)
-                else:
-                    zs[c, k] = (pbuf[c, block] + zr[c, q].astype(F32)).astype(BF)
-                src, dst = zs.at[c, k], zr.at[c, k]
-            send(src, dst, zss.at[c, k], zrs.at[c, k], at_z(sign))
+            lo = 32 * d
+            zs[c, 4 * d, 0:32, :] = part(c, 4)[lo:lo + 32, :].astype(BF)
+            put_z(c, 4 * d, sign, 32)
+            if c in TWO:
+                zs[c, 4 * d + 1] = part(c, 2 * sign)[...].astype(BF)
+                put_z(c, 4 * d + 1, sign)
+
+    def with_half(c, k, d, sign):
+        lo, other = 32 * d, 32 - 32 * d
+        mine = part(c, 3 * sign)
+        got = got_z(c, 4 * d, sign, 32)
+        zs[c, k, lo:lo + 32, :] = (mine[lo:lo + 32, :] + got).astype(BF)
+        zs[c, k, other:other + 32, :] = mine[other:other + 32, :].astype(BF)
+
+    def hop(c, s, d):
+        sign = 1 - 2 * d
+        k = d * 4 + s - 1
+        if s == 2:
+            with_half(c, k, d, sign)
+        else:
+            zs[c, k] = (part(c, sign * (5 - s))[...] + got_z(c, k - 1, sign)).astype(BF)
+        put_z(c, k, sign)
+
+    def pair(c, d):
+        sign = 1 - 2 * d
+        with_half(c, 4 * d + 2, d, sign)
+        put_z(c, 4 * d + 2, 3 * sign)
+        zs[c, 4 * d + 3] = (part(c, sign)[...] + got_z(c, 4 * d + 1, sign)).astype(BF)
+        put_z(c, 4 * d + 3, sign)
 
     lane = lax.broadcasted_iota(jnp.int32, (8, 128), 1)
 
@@ -222,16 +251,9 @@
     adapters_in = [False]
 
     def finish(c):
-        if c == LAST:
-            total = pbuf[c, z]
-            for j in (1, 7, 2, 6, 3, 5, 4):
-                src = lax.rem(z - j + NZ, NZ)
-                remote(zdr.at[src], zdr.at[src], zds.at[j], zdrs.at[j], at_z(j)).wait_recv()
-                total = total + zdr[src].astype(F32)
-        else:
-            for q in (3, 7):
-                remote(zr.at[c, q], zr.at[c, q], zss.at[c, q], zrs.at[c, q], at_z(1)).wait_recv()
-            total = pbuf[c, z] + zr[c, 3].astype(F32) + zr[c, 7].astype(F32)
+        total = pbuf[c, z]
+        for q in (2, 3, 6, 7) if c in TWO else (3, 7):
+            total = total + got_z(c, q, 1)
         b, m = rows_of(ORDER[c])
         keep = jnp.zeros((ROWS, 128), jnp.int32) + alive(m, b // 2)
         total = jnp.where(keep > 0, total, 0.0)
@@ -255,22 +277,23 @@
         own = jnp.concatenate([gall[0], gall[1]], 0)
         both = nt(ug[...].reshape(128, 1024), own).reshape(8, 2, 8, 128)
         keep = of_block(h, alive)[None] > 0
-        part = jnp.where(lane[None] < ROWS, both[:, 0], both[:, 1])
-        plb[...] = jnp.where(keep, part, 0.0)
-        plr[z] = plb[z]
-        for j in range(1, NZ):
-            there = lax.rem(z + j, NZ)
-            send(plb.at[there], plr.at[z], l1s.at[j], l1r.at[j], at_z(j))
+        half = jnp.where(lane[None] < ROWS, both[:, 0], both[:, 1])
+        mine = jnp.where(keep, half, 0.0).reshape(64, 128).astype(BF)
+        plb[...] = mine
+        plr[z] = mine
+        for j in (4, 3, 5, 2, 6, 1, 7):
+            send(plb, plr.at[z], l1s.at[j], l1r.at[j], at_z(j))
 
     def rank_sum():
         for j in range(1, NZ):
             src = lax.rem(z - j + NZ, NZ)
             remote(plr.at[src], plr.at[src], l1s.at[j], l1r.at[j], at_z(j)).wait_recv()
-        total = jnp.sum(plr[...], 0).astype(BF).astype(F32)
-        l2b[...] = total
-        l2r[z] = total
-        for j in range(1, NZ):
-            send(l2b, l2r.at[z], l2s.at[j], l2rs.at[j], at_z(j))
+        mine = jnp.sum(plr[...].astype(F32), 0).astype(BF)
+        l3b[...] = mine
+        lfull[h] = mine
+        send(l3b, lfull.at[h], l3s.at[0], l3r.at[0], at_y)
+        for j in range(1, NX):
+            send(l3b, lfull.at[h], l3s.at[j], l3r.at[j], at_x(j))
         for j in range(1, NZ):
             src = lax.rem(z - j + NZ, NZ)
             remote(hz.at[src], hz.at[src], h1s.at[j], h1r.at[j], at_z(j)).wait_recv()
@@ -284,17 +307,6 @@
         for j in range(1, NX):
             there = yh * NX + lax.rem(x + j, NX)
             send(hkb.at[there], hk.at[h], h2s.at[j], h2r.at[j], at_x(j))
-
-    def rank_spread():
-        for j in range(1, NZ):
-            src = lax.rem(z - j + NZ, NZ)
-            remote(l2r.at[src], l2r.at[src], l2s.at[j], l2rs.at[j], at_z(j)).wait_recv()
-        mine = l2r[...].reshape(64, 128).astype(BF)
-        l3b[...] = mine
-        lfull[h] = mine
-        send(l3b, lfull.at[h], l3s.at[0], l3r.at[0], at_y)
-        for j in range(1, NX):
-            send(l3b, lfull.at[h], l3s.at[j], l3r.at[j], at_x(j))
 
     def rank_relay():
         remote(lfull.at[hp], lfull.at[hp], l3s.at[0], l3r.at[0], at_y).wait_recv()
@@ -353,52 +365,38 @@
             right = jnp.concatenate(
                 [xv[0, b * ROWS:(b + 1) * ROWS], xv[1, b * ROWS:(b + 1) * ROWS]], 0
             )
-            part = nn(left, right)
+            term = nn(left, right)
             if b == 0:
-                dacc[...] = part
+                dacc[...] = term
             elif b < NH - 1:
-                dacc[...] += part
+                dacc[...] += term
             else:
-                da_ref[...] = (dacc[...] + part).astype(BF)
+                da_ref[...] = (dacc[...] + term).astype(BF)
 
     loads[2].wait()
     done = []
-    for step in range(N + 4 * LAG):
-        c = step - 4 * LAG
-        if 0 <= c:
-            finish(c)
-            if not adapters_in[0]:
-                done.append(c)
-        for s in (4, 3, 2):
-            if 0 <= step - LAG * (s - 1) < LAST:
-                hop(step - LAG * (s - 1), s)
-        for name, half in EARLY.get(step, ()):
-            arrive(name, (half,))
-        if step < N:
-            arrive(ORDER[step])
-            prod = nt(gall[step], wv[...])
-            for j in range(NZ):
-                pbuf[step, j] = prod[:, j * 128:(j + 1) * 128]
-            if step == LAST:
-                direct()
-            else:
-                hop(step, 1)
-        if step == EVENTS["up_relay"]:
-            up_relay()
-        if step == EVENTS["up_rows"]:
-            up_rows()
-        if step == EVENTS["rank_sum"]:
-            rank_sum()
-        if step == EVENTS["rank_spread"]:
-            rank_spread()
-        if step == EVENTS["rank_relay"]:
-            rank_relay()
-        if step == EVENTS["rank_here"]:
-            rank_here(tuple(done))
-        if step == EVENTS["up_gradient"]:
-            up_gradient()
-        if step == EVENTS["down_gradient"]:
-            down_gradient()
+
+    def multiply(c):
+        arrive(ORDER[c])
+        prod = nt(gall[c], wv[...])
+        for j in range(NZ):
+            pbuf[c, j] = prod[:, j * 128:(j + 1) * 128]
+        first(c)
+
+    def close(c):
+        finish(c)
+        if not adapters_in[0]:
+            done.append(c)
+
+    does = {
+        "fwd": lambda name, half: arrive(name, (half,)),
+        "mm": multiply, "hop": hop, "pair": pair, "fin": close,
+        "up_relay": up_relay, "up_rows": up_rows, "rank_sum": rank_sum,
+        "rank_relay": rank_relay, "rank_here": lambda: rank_here(tuple(done)),
+        "up_gradient": up_gradient, "down_gradient": down_gradient,
+    }
+    for what, *which in PLAN:
+        does[what](*which)
 
     for c in range(N):
         b, m = rows_of(ORDER[c])
@@ -408,52 +406,66 @@
         copy.wait_send()
 
 
+def hand_out(out, da, du, out_to, da_to, du_to):
+    out_to[...] = out[...]
+    da_to[...] = da[...]
+    du_to[...] = du[...]
+
+
 def shards(
     output_gradient, forward_input, saved_rank_outputs, projection_weight,
     adapter_down_maps, adapter_up_maps, segment_adapter_class, live_segment_table,
 ):
     vm = pltpu.VMEM
     dma = pltpu.SemaphoreType.DMA
-    smem = pl.BlockSpec(memory_space=pltpu.SMEM)
     vmem = pl.BlockSpec(memory_space=pltpu.VMEM)
     hbm = pl.BlockSpec(memory_space=pl.ANY)
-    out, da, du = pl.pallas_call(
+    shapes = (
+        jax.ShapeDtypeStruct((2, 512, 128), BF),
+        jax.ShapeDtypeStruct((512, 128), BF),
+        jax.ShapeDtypeStruct((64, 1024), BF),
+    )
+    outs = pl.pallas_call(
         section,
         name="section",
-        out_shape=(
-            jax.ShapeDtypeStruct((2, 512, 128), BF),
-            jax.ShapeDtypeStruct((512, 128), BF),
-            jax.ShapeDtypeStruct((64, 1024), BF),
-        ),
-        in_specs=[smem, smem, hbm, hbm, hbm, hbm, hbm, hbm],
+        out_shape=shapes,
+        in_specs=[hbm, hbm, hbm, hbm, hbm, hbm, hbm, hbm],
         out_specs=(vmem, vmem, vmem),
         scratch_shapes=[
             vm((N, ROWS, 1024), BF), vm((1024, 1024), BF), vm((N, 8, ROWS, 128), F32),
             vm((N, 8, ROWS, 128), BF), vm((N, 8, ROWS, 128), BF),
             vm((8, 8, 1024), F32), vm((4, 16, 1024), BF), vm((8, 16, 1024), BF),
-            vm((8, 8, 128), F32), vm((8, 8, 128), F32), vm((8, 128), F32), vm((8, 8, 128), F32),
-            vm((64, 128), BF), vm((8, 64, 128), BF), vm((N, ROWS, 128), F32),
+            vm((64, 128), BF), vm((8, 64, 128), BF), vm((64, 128), BF), vm((8, 64, 128), BF),
+            vm((N, ROWS, 128), F32),
             vm((8, 2, 8, 64), BF), vm((8, 8, 128), F32), vm((8, 8, 128), F32),
             vm((2, 512, 128), BF), vm((8, 64, 128), BF), vm((N, ROWS, 128), BF), vm((512, 128), F32),
             vm((64, 1024), BF), vm((2, 8, 64), BF),
-            vm((2, 16, 1024), BF), vm((4, 8, 128), F32), vm((8, ROWS, 128), BF), vm((8, ROWS, 128), BF),
-            dma((7,)), dma((32,)), dma((N, 2)), dma((N, 8)), dma((N, 8)),
+            vm((2, 16, 1024), BF), vm((4, 8, 128), F32),
+            pltpu.SMEM((1, 2, 4), jnp.int32), pltpu.SMEM((1, 2), jnp.int32),
+            dma((9,)), dma((32,)), dma((N, 2)), dma((N, 8)), dma((N, 8)),
             dma((8,)), dma((8,)), dma((8,)), dma((8,)), dma((8,)), dma((8,)),
-            dma((8,)), dma((8,)), dma((8,)), dma((8,)), dma((8,)), dma((8,)), dma((N,)), dma((N,)), dma((8,)), dma((8,)),
+            dma((8,)), dma((8,)), dma((8,)), dma((8,)), dma((N,)), dma((N,)),
         ],
         compiler_params=pltpu.CompilerParams(
-            collective_id=0, has_side_effects=True, vmem_limit_bytes=67043328
+            collective_id=0, has_side_effects=True, vmem_limit_bytes=40 * 1024 * 1024
         ),
     )(
-        segment_adapter_class,
-        live_segment_table,
-        output_gradient.reshape(2, ROWS, 1024),
-        forward_input.reshape(2, 512, 128),
-        saved_rank_outputs.reshape(2, 8, 64),
-        projection_weight.reshape(1024, 1024),
-        adapter_down_maps.reshape(8, 64, 128),
-        adapter_up_maps.reshape(64, 1024),
+        pltpu.with_memory_space_constraint(segment_adapter_class, pltpu.HBM),
+        pltpu.with_memory_space_constraint(live_segment_table, pltpu.HBM),
+        pltpu.with_memory_space_constraint(output_gradient.reshape(2, ROWS, 1024), pltpu.HBM),
+        pltpu.with_memory_space_constraint(forward_input.reshape(2, 512, 128), pltpu.HBM),
+        pltpu.with_memory_space_constraint(saved_rank_outputs.reshape(2, 8, 64), pltpu.HBM),
+        pltpu.with_memory_space_constraint(projection_weight.reshape(1024, 1024), pltpu.HBM),
+        pltpu.with_memory_space_constraint(adapter_down_maps.reshape(8, 64, 128), pltpu.HBM),
+        pltpu.with_memory_space_constraint(adapter_up_maps.reshape(64, 1024), pltpu.HBM),
     )
+    out, da, du = pl.pallas_call(
+        hand_out,
+        name="hand_out",
+        out_shape=shapes,
+        in_specs=[vmem] * 3,
+        out_specs=(vmem,) * 3,
+    )(*[pltpu.with_memory_space_constraint(o, pltpu.VMEM) for o in outs])
     return (
         out.reshape(1, 2, 512, 128),
         da.reshape(1, 8, 64, 128),

time: 76 us -> 65.4 us (0.86)
  Pallas kernels: 70.4 us -> 64.6 us
  local copies, waits for them, and re-layouts: 4.8 us -> 0 us
    pallas_call x1 -> x2, Pallas kernels: 70.4 us -> 64.6 us  [the longest x1 63.8 us: shards(): pl.pallas_call(section, name='section', out_shape=shapes, in_specs=[hbm,...]
    unnamed x3 -> x0, local copies, waits for them, and re-layouts: 4.8 us -> none
where the time goes in v3:
time: 65.4 us; the launch traced here: 65.2 us
  Pallas kernels  64.6 us (99%)
    pallas_call x1, Pallas kernels, shards(): pl.pallas_call(section, name='section', out_shape=shapes, in_specs=[hbm,...  63.8 us

profile of v3, /device:TPU:1, one launch (start us, length us, event | category | flops | bytes accessed | tf_op | source)
XLA Modules:
  0.0 65.2 jit_solution(14573566450218371225)
XLA Ops:
  0.6 63.8 %section.1 = (bf16[2,512,128]{2,1,0:T(8,128)(2,1)S(1)}, bf16[512,128]{1,0:T(8,128)(2,1)S(1)}, bf16[64,1024]{1,0:T(8,128)(2,1)S(1)}) custom-call(s32[1,2,4]{2,1,0:T(2,128)} %cls_at.1, s32[1,2]{1,0:T(1,128)} %live_at.1, bf16[2,64,1024]{2,1,0:T(8,128)(2,1)} %bitcast.10, bf16[2,512,128]{2,1,0:T(8,128)(2,1)} %bitcast.11, bf16[2,8,64]{2,1,0:T(8,128)(2,1)} %bitcast.14, ...), custom_call_target="tpu_custom_call" | custom-call | tf_op jit(solution)/shard_map/section/pallas_call | solution.py:428
  64.4 0.8 %hand_out.1 = (bf16[2,512,128]{2,1,0:T(8,128)(2,1)}, bf16[512,128]{1,0:T(8,128)(2,1)}, bf16[64,1024]{1,0:T(8,128)(2,1)}) custom-call(bf16[2,512,128]{2,1,0:T(8,128)(2,1)S(1)} %get-tuple-element.9.out, bf16[512,128]{1,0:T(8,128)(2,1)S(1)} %get-tuple-element.10.da, bf16[64,1024]{1,0:T(8,128)(2,1)S(1)} %get-tuple-element.11.du), custom_call_target="tpu_custom_call" | custom-call | tf_op jit(solution)/shard_map/hand_out/pallas_call | solution.py:462

commit v4 on v3

--- a/solution.py
+++ b/solution.py
@@ -16,7 +16,7 @@
 )
 SLOT = {name: i for i, name in enumerate(ORDER)}
 N = len(ORDER)
-TWO = (13, 14, 15)
+TWO = (7, 13, 14, 15)
 SHIFT = {"O": 0, "L": 3, "R": 1, "X": 2, "Y": 0, "YL": 3, "YR": 1, "YX": 2}
 ONWARD = {
     ("L0", 0): ((1, "X0"),),
@@ -24,37 +24,34 @@
     ("R0", 1): ((-1, "X0"),),
     ("R1", 1): ((-1, "X1"),),
     ("Y0", 0): ((1, "YL0"), (-1, "YR0")),
-    ("Y0", 1): ((1, "YL0"), (-1, "YR0")),
+    ("Y0", 1): ((1, "YL0"), (-1, "YR0"), (2, "YX0")),
     ("Y1", 0): ((1, "YL1"), (-1, "YR1")),
     ("Y1", 1): ((1, "YL1"), (-1, "YR1"), (2, "YX1")),
     ("YL0", 0): ((1, "YX0"),),
     ("YL1", 0): ((1, "YX1"),),
-    ("YR0", 1): ((-1, "YX0"),),
 }
 PLAN = (
-    ("mm", 0), ("mm", 1), ("hop", 0, 2, 0), ("hop", 0, 2, 1), ("fwd", "L0", 0), ("hop", 1, 2, 0),
-    ("hop", 1, 2, 1), ("fwd", "R0", 1), ("mm", 2), ("mm", 3), ("fwd", "L1", 0), ("hop", 0, 3, 0),
-    ("hop", 0, 3, 1), ("hop", 1, 3, 0), ("up_relay",), ("hop", 1, 3, 1), ("fwd", "R1", 1), ("mm", 4),
-    ("mm", 5), ("hop", 2, 2, 0), ("hop", 2, 2, 1), ("hop", 3, 2, 0), ("hop", 3, 2, 1), ("hop", 0, 4, 0),
-    ("fwd", "Y0", 0), ("hop", 0, 4, 1), ("hop", 1, 4, 0), ("hop", 1, 4, 1), ("mm", 6), ("hop", 4, 2, 0),
-    ("hop", 4, 2, 1), ("hop", 5, 2, 0), ("hop", 5, 2, 1), ("hop", 2, 3, 0), ("hop", 2, 3, 1),
-    ("fwd", "Y0", 1), ("mm", 8), ("hop", 3, 3, 0), ("hop", 3, 3, 1), ("fin", 0), ("up_rows",),
-    ("fwd", "YL0", 0), ("fin", 1), ("hop", 6, 2, 0), ("hop", 6, 2, 1), ("mm", 7), ("fwd", "Y1", 0),
-    ("hop", 4, 3, 0), ("hop", 2, 4, 0), ("hop", 2, 4, 1), ("hop", 4, 3, 1), ("hop", 5, 3, 0),
-    ("hop", 5, 3, 1), ("hop", 8, 2, 0), ("hop", 8, 2, 1), ("hop", 3, 4, 0), ("hop", 3, 4, 1), ("mm", 9),
-    ("fwd", "YR0", 1), ("mm", 10), ("fwd", "Y1", 1), ("mm", 11), ("fwd", "YL1", 0), ("hop", 6, 3, 0),
-    ("hop", 6, 3, 1), ("hop", 7, 2, 0), ("hop", 7, 2, 1), ("hop", 4, 4, 0), ("hop", 4, 4, 1), ("fin", 2),
-    ("hop", 5, 4, 0), ("hop", 5, 4, 1), ("mm", 12), ("rank_sum",), ("hop", 8, 3, 0), ("hop", 8, 3, 1),
-    ("hop", 9, 2, 0), ("hop", 9, 2, 1), ("hop", 10, 2, 0), ("hop", 10, 2, 1), ("hop", 11, 2, 0),
-    ("hop", 11, 2, 1), ("hop", 6, 4, 0), ("hop", 6, 4, 1), ("fin", 3), ("hop", 7, 3, 0), ("hop", 7, 3, 1),
-    ("mm", 13), ("fin", 4), ("fin", 5), ("mm", 14), ("hop", 12, 2, 0), ("hop", 12, 2, 1), ("mm", 15),
-    ("hop", 8, 4, 0), ("hop", 8, 4, 1), ("hop", 9, 3, 0), ("hop", 9, 3, 1), ("hop", 10, 3, 0),
-    ("hop", 10, 3, 1), ("hop", 11, 3, 0), ("hop", 11, 3, 1), ("fin", 6), ("hop", 7, 4, 0), ("hop", 7, 4, 1),
-    ("pair", 13, 0), ("pair", 13, 1), ("rank_relay",), ("pair", 14, 0), ("hop", 12, 3, 0), ("hop", 12, 3, 1),
-    ("pair", 14, 1), ("pair", 15, 0), ("pair", 15, 1), ("fin", 8), ("hop", 9, 4, 0), ("hop", 9, 4, 1),
-    ("hop", 10, 4, 0), ("hop", 10, 4, 1), ("hop", 11, 4, 0), ("hop", 11, 4, 1), ("fin", 7), ("hop", 12, 4, 1),
-    ("rank_here",), ("hop", 12, 4, 0), ("fin", 13), ("down_gradient",), ("fin", 14), ("fin", 9),
-    ("up_gradient",), ("fin", 10), ("fin", 11), ("fin", 15), ("fin", 12),
+    ("mm", 0, 1), ("hop", 0, 2, 0), ("hop", 0, 2, 1), ("hop", 1, 2, 1), ("hop", 1, 2, 0), ("fwd", "L0", 0),
+    ("fwd", "R0", 1), ("mm", 2, 3), ("hop", 0, 3, 0), ("hop", 0, 3, 1), ("fwd", "L1", 0), ("hop", 1, 3, 0),
+    ("hop", 1, 3, 1), ("up_relay",), ("fwd", "R1", 1), ("mm", 4, 5), ("hop", 2, 2, 0), ("hop", 2, 2, 1),
+    ("hop", 3, 2, 1), ("hop", 3, 2, 0), ("hop", 0, 4, 0), ("hop", 0, 4, 1), ("hop", 1, 4, 0),
+    ("hop", 1, 4, 1), ("fwd", "Y0", 0), ("mm", 6), ("hop", 4, 2, 0), ("hop", 5, 2, 0), ("hop", 2, 3, 0),
+    ("hop", 5, 2, 1), ("hop", 2, 3, 1), ("hop", 3, 3, 0), ("hop", 3, 3, 1), ("hop", 4, 2, 1),
+    ("fwd", "Y0", 1), ("mm", 8), ("fin", 1), ("fin", 0), ("up_rows",), ("fwd", "YL0", 0), ("hop", 6, 2, 0),
+    ("hop", 6, 2, 1), ("hop", 4, 3, 0), ("hop", 5, 3, 1), ("hop", 5, 3, 0), ("fwd", "Y1", 0), ("mm", 7),
+    ("hop", 2, 4, 1), ("hop", 8, 2, 0), ("hop", 4, 3, 1), ("hop", 3, 4, 0), ("hop", 2, 4, 0),
+    ("hop", 3, 4, 1), ("hop", 8, 2, 1), ("mm", 9, 10), ("fwd", "Y1", 1), ("mm", 11), ("mm", 12),
+    ("hop", 6, 3, 0), ("hop", 5, 4, 1), ("hop", 4, 4, 0), ("hop", 6, 3, 1), ("hop", 5, 4, 0), ("pair", 7, 1),
+    ("fwd", "YL1", 0), ("pair", 7, 0), ("hop", 8, 3, 0), ("hop", 4, 4, 1), ("rank_sum",), ("fin", 2),
+    ("hop", 9, 2, 0), ("hop", 10, 2, 1), ("hop", 10, 2, 0), ("hop", 9, 2, 1), ("hop", 8, 3, 1),
+    ("hop", 12, 2, 0), ("hop", 12, 2, 1), ("hop", 11, 2, 0), ("hop", 6, 4, 0), ("hop", 11, 2, 1),
+    ("mm", 13, 14), ("hop", 6, 4, 1), ("fin", 5), ("fin", 3), ("mm", 15), ("hop", 8, 4, 0), ("hop", 10, 3, 1),
+    ("fin", 4), ("hop", 9, 3, 1), ("hop", 9, 3, 0), ("hop", 10, 3, 0), ("hop", 8, 4, 1), ("hop", 12, 3, 0),
+    ("hop", 12, 3, 1), ("fin", 7), ("hop", 11, 3, 0), ("hop", 11, 3, 1), ("rank_relay",), ("pair", 13, 1),
+    ("pair", 13, 0), ("pair", 14, 1), ("pair", 14, 0), ("fin", 6), ("pair", 15, 0), ("pair", 15, 1),
+    ("hop", 10, 4, 1), ("hop", 9, 4, 0), ("hop", 9, 4, 1), ("hop", 10, 4, 0), ("fin", 8), ("hop", 12, 4, 0),
+    ("hop", 12, 4, 1), ("hop", 11, 4, 0), ("hop", 11, 4, 1), ("rank_here",), ("down_gradient",), ("fin", 13),
+    ("up_gradient",), ("fin", 14), ("fin", 9), ("fin", 10), ("fin", 12), ("fin", 15), ("fin", 11),
 )
 
 
@@ -69,7 +66,7 @@
 def section(
     cls_at, live_at, g_ref, x_ref, hid_ref, w_ref, a_ref, u_ref,
     out_ref, da_ref, du_ref,
-    gall, wv, pbuf, zs, zr, uf, us, ug, plb, plr, l3b, lfull, lt,
+    gall, wv, wt, pbuf, zs, zr, uf, us, ug, plb, plr, l3b, lfull, lt,
     hz, hkb, hk, xv, av, fin, dacc, uv, hidv, uy, hy, cls_ref, live_ref,
     loc, gss, grs, zss, zrs, uss, urs, l1s, l1r, l3s, l3r, h1s, h1r, h2s, h2r, fs, fr,
 ):
@@ -131,6 +128,8 @@
     ug[h] = us[h // 2]
     hz[z] = hidv[...]
 
+    loads[2].wait()
+    wt[...] = wv[...].T
     pl.semaphore_wait(bar, 13)
 
     sends = []
@@ -373,15 +372,16 @@
             else:
                 da_ref[...] = (dacc[...] + term).astype(BF)
 
-    loads[2].wait()
     done = []
 
-    def multiply(c):
-        arrive(ORDER[c])
-        prod = nt(gall[c], wv[...])
-        for j in range(NZ):
-            pbuf[c, j] = prod[:, j * 128:(j + 1) * 128]
-        first(c)
+    def multiply(*chunks):
+        for c in chunks:
+            arrive(ORDER[c])
+        prod = nn(jnp.concatenate([gall[c] for c in chunks], 0), wt[...])
+        for i, c in enumerate(chunks):
+            for j in range(NZ):
+                pbuf[c, j] = prod[i * ROWS:(i + 1) * ROWS, j * 128:(j + 1) * 128]
+            first(c)
 
     def close(c):
         finish(c)
@@ -432,7 +432,7 @@
         in_specs=[hbm, hbm, hbm, hbm, hbm, hbm, hbm, hbm],
         out_specs=(vmem, vmem, vmem),
         scratch_shapes=[
-            vm((N, ROWS, 1024), BF), vm((1024, 1024), BF), vm((N, 8, ROWS, 128), F32),
+            vm((N, ROWS, 1024), BF), vm((1024, 1024), BF), vm((1024, 1024), BF), vm((N, 8, ROWS, 128), F32),
             vm((N, 8, ROWS, 128), BF), vm((N, 8, ROWS, 128), BF),
             vm((8, 8, 1024), F32), vm((4, 16, 1024), BF), vm((8, 16, 1024), BF),
             vm((64, 128), BF), vm((8, 64, 128), BF), vm((64, 128), BF), vm((8, 64, 128), BF),

time: 65.4 us -> 62.8 us (0.960)
  Pallas kernels: 64.6 us -> 62 us
    pallas_call x1, Pallas kernels: 63.8 us -> 61.2 us  [shards(): pl.pallas_call(section, name='section', out_shape=shapes, in_specs=[hbm,...]
where the time goes in v4:
time: 62.8 us; the launch traced here: 62.6 us
  Pallas kernels  62 us (99%)
  between operations  0.64 us (1%)
    pallas_call x1, Pallas kernels, shards(): pl.pallas_call(section, name='section', out_shape=shapes, in_specs=[hbm,...  61.2 us

profile of v4, /device:TPU:1, one launch (start us, length us, event | category | flops | bytes accessed | tf_op | source)
XLA Modules:
  0.0 62.6 jit_solution(18118414856352418749)
XLA Ops:
  0.6 61.2 %section.1 = (bf16[2,512,128]{2,1,0:T(8,128)(2,1)S(1)}, bf16[512,128]{1,0:T(8,128)(2,1)S(1)}, bf16[64,1024]{1,0:T(8,128)(2,1)S(1)}) custom-call(s32[1,2,4]{2,1,0:T(2,128)} %cls_at.1, s32[1,2]{1,0:T(1,128)} %live_at.1, bf16[2,64,1024]{2,1,0:T(8,128)(2,1)} %bitcast.10, bf16[2,512,128]{2,1,0:T(8,128)(2,1)} %bitcast.11, bf16[2,8,64]{2,1,0:T(8,128)(2,1)} %bitcast.14, ...), custom_call_target="tpu_custom_call" | custom-call | tf_op jit(solution)/shard_map/section/pallas_call | solution.py:428
  61.8 0.8 %hand_out.1 = (bf16[2,512,128]{2,1,0:T(8,128)(2,1)}, bf16[512,128]{1,0:T(8,128)(2,1)}, bf16[64,1024]{1,0:T(8,128)(2,1)}) custom-call(bf16[2,512,128]{2,1,0:T(8,128)(2,1)S(1)} %get-tuple-element.9.out, bf16[512,128]{1,0:T(8,128)(2,1)S(1)} %get-tuple-element.10.da, bf16[64,1024]{1,0:T(8,128)(2,1)S(1)} %get-tuple-element.11.du), custom_call_target="tpu_custom_call" | custom-call | tf_op jit(solution)/shard_map/hand_out/pallas_call | solution.py:462

commit v5 on v4

--- a/solution.py
+++ b/solution.py
@@ -50,8 +50,8 @@
     ("hop", 12, 3, 1), ("fin", 7), ("hop", 11, 3, 0), ("hop", 11, 3, 1), ("rank_relay",), ("pair", 13, 1),
     ("pair", 13, 0), ("pair", 14, 1), ("pair", 14, 0), ("fin", 6), ("pair", 15, 0), ("pair", 15, 1),
     ("hop", 10, 4, 1), ("hop", 9, 4, 0), ("hop", 9, 4, 1), ("hop", 10, 4, 0), ("fin", 8), ("hop", 12, 4, 0),
-    ("hop", 12, 4, 1), ("hop", 11, 4, 0), ("hop", 11, 4, 1), ("rank_here",), ("down_gradient",), ("fin", 13),
-    ("up_gradient",), ("fin", 14), ("fin", 9), ("fin", 10), ("fin", 12), ("fin", 15), ("fin", 11),
+    ("hop", 12, 4, 1), ("hop", 11, 4, 0), ("hop", 11, 4, 1), ("rank_here",), ("fin", 13), ("fin", 14),
+    ("fin", 9), ("fin", 10), ("fin", 12), ("fin", 15), ("fin", 11), ("up_gradient",), ("down_gradient",),
 )
 
 
@@ -128,8 +128,6 @@
     ug[h] = us[h // 2]
     hz[z] = hidv[...]
 
-    loads[2].wait()
-    wt[...] = wv[...].T
     pl.semaphore_wait(bar, 13)
 
     sends = []
@@ -372,6 +370,8 @@
             else:
                 da_ref[...] = (dacc[...] + term).astype(BF)
 
+    loads[2].wait()
+    wt[...] = wv[...].T
     done = []
 
     def multiply(*chunks):

time: 62.8 us -> 61.6 us (0.981)
  Pallas kernels: 62 us -> 60.8 us
    pallas_call x1, Pallas kernels: 61.2 us -> 60 us  [shards(): pl.pallas_call(section, name='section', out_shape=shapes, in_specs=[hbm,...]
where the time goes in v5:
time: 61.6 us; the launch traced here: 61.5 us
  Pallas kernels  60.8 us (99%)
  between operations  0.64 us (1%)
    pallas_call x1, Pallas kernels, shards(): pl.pallas_call(section, name='section', out_shape=shapes, in_specs=[hbm,...  60 us

profile of v5, /device:TPU:1, one launch (start us, length us, event | category | flops | bytes accessed | tf_op | source)
XLA Modules:
  0.0 61.5 jit_solution(3163290272028933418)
XLA Ops:
  0.6 60.0 %section.1 = (bf16[2,512,128]{2,1,0:T(8,128)(2,1)S(1)}, bf16[512,128]{1,0:T(8,128)(2,1)S(1)}, bf16[64,1024]{1,0:T(8,128)(2,1)S(1)}) custom-call(s32[1,2,4]{2,1,0:T(2,128)} %cls_at.1, s32[1,2]{1,0:T(1,128)} %live_at.1, bf16[2,64,1024]{2,1,0:T(8,128)(2,1)} %bitcast.10, bf16[2,512,128]{2,1,0:T(8,128)(2,1)} %bitcast.11, bf16[2,8,64]{2,1,0:T(8,128)(2,1)} %bitcast.14, ...), custom_call_target="tpu_custom_call" | custom-call | tf_op jit(solution)/shard_map/section/pallas_call | solution.py:428
  60.6 0.8 %hand_out.1 = (bf16[2,512,128]{2,1,0:T(8,128)(2,1)}, bf16[512,128]{1,0:T(8,128)(2,1)}, bf16[64,1024]{1,0:T(8,128)(2,1)}) custom-call(bf16[2,512,128]{2,1,0:T(8,128)(2,1)S(1)} %get-tuple-element.9.out, bf16[512,128]{1,0:T(8,128)(2,1)S(1)} %get-tuple-element.10.da, bf16[64,1024]{1,0:T(8,128)(2,1)S(1)} %get-tuple-element.11.du), custom_call_target="tpu_custom_call" | custom-call | tf_op jit(solution)/shard_map/hand_out/pallas_call | solution.py:462
